TPU v7x, 128 devices: a whole 4x4x4 slice. The times are simulated.
128 devices in a mesh: grp: 4 (over x), dev: 32 (over z, y, core).
Axes of the slice: x: 4, y: 4, z: 4, core: 2. Of those that a mesh axis runs over, the one named last changes fastest.
Arguments:
- image_tokens: bfloat16 [512, 197, 768], P(('grp', 'dev')), may hold values from -64 to 64
- text_tokens: bfloat16 [512, 30, 768], P(('grp', 'dev')), may hold values from -64 to 64
- negatives: int32 [512, 2], P(('grp', 'dev')), may hold values from 0 to 127, as said below
- query_weight: bfloat16 [768, 768], replicated, may hold values from -0.21875 to 0.21875
- kv_weight: bfloat16 [768, 1536], replicated, may hold values from -0.21875 to 0.21875
- match_head: float32 [768], replicated, may hold values from -6 to 6
- cotangent: bfloat16 [512, 3], P(('grp', 'dev')), may hold values from -6 to 6
Outputs:
- logits: float32 [512, 3], P(('grp', 'dev'))
- grad_query_weight: float32 [768, 768], P(('grp', 'dev'))
- grad_kv_weight: float32 [768, 1536], P(('grp', 'dev'))
Inputs may be any that keep to these rules, and one draw needn't show every extreme that they name: At most 2 of the 8 negatives of one device lie on any one device of its group, and in every group some device holds exactly 2 negatives of every device of the group.
All inputs are finite; a program needn't handle non-finite values.
Results may differ from a plain program's by a relative error of at most 0.0085.
The roundings to bfloat16 on the way count: a program that leaves them out, or rounds other values in their place, can miss the bound.
Values may be sent and summed in bfloat16 or wider, within the bound.
No kernel may reach another device: no remote copies, remote signals or barrier semaphores. Data moves between devices by JAX's collectives and lax.ppermute only.
A program may use at most 128 MiB of HBM per device.

v0:
```python
import functools

import jax
import jax.numpy as jnp
from jax import lax
from jax.experimental import pallas as pl
from jax.experimental.pallas import tpu as pltpu
from jax.sharding import Mesh
from jax.sharding import PartitionSpec as P


DEV = ("dev_0", "dev_1", "dev_2")
GRP_DEV = ("grp", "dev_0", "dev_1", "dev_2")
RINGS = ("grp", "dev_0", "dev_1")
ORDERS = ((0, 2, 1), (1, 2, 0), (2, 1, 0))

D = 768
LI = 197
LP = 200
LX = 256
LT = 30
QP = 32
GROUPS = 3
GW = 256
ROWS = 128
F32 = jnp.float32
BF16 = jnp.bfloat16


def nn(a, b):
    return lax.dot_general(a, b, (((1,), (0,)), ((), ())), preferred_element_type=F32)


def nt(a, b):
    return lax.dot_general(a, b, (((1,), (1,)), ((), ())), preferred_element_type=F32)


def tn(a, b):
    return lax.dot_general(a, b, (((0,), (0,)), ((), ())), preferred_element_type=F32)


def block_mask():
    row = lax.broadcasted_iota(jnp.int32, (ROWS, GW), 0)
    col = lax.broadcasted_iota(jnp.int32, (ROWS, GW), 1)
    return row, (row // QP) == (col // 64)


def fill_constants(head_ref, mhx_ref, ones_ref):
    row, same = block_mask()
    ones_ref[...] = jnp.where(same & (row % QP < LT), 1.0, 0.0).astype(BF16)
    for g in range(GROUPS):
        rest = head_ref[:, g * GW : (g + 1) * GW]
        for piece in range(3):
            part = rest.astype(BF16)
            rest = rest - part.astype(F32)
            wide = jnp.broadcast_to(part.astype(F32), (ROWS, GW))
            mhx_ref[piece * GROUPS + g] = jnp.where(same, wide, 0.0).astype(BF16)


def attend_pair(i, row, text, scale, keyval, qx_ref, head_ref, mhx_ref, ones_ref, dkv_ref, dq_ref, lrow_ref):
    tail = lax.broadcasted_iota(jnp.int32, (8, ROWS), 0) < (LI - (LP - 8))
    base = pl.multiple_of(i * LX, LX)
    trow = pl.multiple_of(text * QP, QP)
    total = jnp.zeros((1, GW), F32)
    for g in range(GROUPS):
        lo = g * GW
        keys = keyval(lo)
        values = keyval(D + lo)
        query = qx_ref[text * GROUPS + g]
        head = head_ref[:, lo : lo + GW]
        scores = nt(keys, query)
        scores = jnp.concatenate(
            [scores[: LP - 8], jnp.where(tail, scores[LP - 8 :], -1e30)], axis=0
        )
        top = jnp.max(scores, axis=0, keepdims=True)
        expd = jnp.exp(scores - top)
        probs = expd * (1.0 / jnp.sum(expd, axis=0, keepdims=True))
        probs_low = probs.astype(BF16)
        dp = nt(values, mhx_ref[g]) + nt(values, mhx_ref[GROUPS + g]) + nt(values, mhx_ref[2 * GROUPS + g])
        dp = dp * scale
        mean = jnp.sum(probs * dp, axis=0, keepdims=True)
        d_low = (probs * (dp - mean)).astype(BF16)
        dkv_ref[pl.ds(base, LP), lo : lo + GW] = nn(d_low, query).astype(BF16)
        weight = nn(probs_low, ones_ref[...])
        dkv_ref[pl.ds(base, LP), D + lo : D + lo + GW] = (weight * (head * scale)).astype(BF16)
        total = total + jnp.sum(weight * values.astype(F32), axis=0, keepdims=True) * head
        wide = tn(d_low, keys)
        col = lax.broadcasted_iota(jnp.int32, (QP, GW), 1) // 64
        dq = jnp.where(col == 0, wide[:QP], 0.0)
        for h in range(1, 4):
            dq = jnp.where(col == h, wide[h * QP : (h + 1) * QP], dq)
        dq_ref[pl.ds(trow, QP), lo : lo + GW] += dq * 0.125
    lrow_ref[pl.ds(row, 1), :] = total


def own_kernel(
    tan_ref, text_ref, qw_ref, image_ref, kvw_ref, head_ref,
    qx_ref, mhx_ref, ones_ref, grad_ref, dq_ref, lrow_ref,
    kv_ref, dkv_ref, xt_ref,
    *, pairs,
):
    fill_constants(head_ref, mhx_ref, ones_ref)
    dq_ref[...] = jnp.zeros_like(dq_ref)
    dkv_ref[...] = jnp.zeros_like(dkv_ref)
    queries = (nn(text_ref[...], qw_ref[...]).astype(BF16).astype(F32) * 0.125)
    _, same = block_mask()
    for t in range(pairs):
        for g in range(GROUPS):
            part = queries[t * QP : (t + 1) * QP, g * GW : (g + 1) * GW]
            wide = jnp.concatenate([part] * 4, axis=0)
            qx_ref[t * GROUPS + g] = jnp.where(same, wide, 0.0).astype(BF16)

    def one(i, carry):
        image = image_ref[i]
        kv_ref[...] = nn(image, kvw_ref[...]).astype(BF16)
        wide = jnp.concatenate([image, jnp.zeros((LX - LP, D), BF16)], axis=0)
        xt_ref[:, pl.ds(pl.multiple_of(i * LX, LX), LX)] = wide.T
        attend_pair(
            i, i, i, tan_ref[i], lambda lo: kv_ref[:, lo : lo + GW],
            qx_ref, head_ref, mhx_ref, ones_ref, dkv_ref, dq_ref, lrow_ref,
        )
        return carry

    lax.fori_loop(0, pairs, one, 0)

    def block(n, carry):
        cols = pl.ds(pl.multiple_of(n * GW, GW), GW)
        grad_ref[:, cols] = nn(xt_ref[...], dkv_ref[:, cols])
        return carry

    lax.fori_loop(0, 2 * D // GW, block, 0)


def strip_rows(color, rings):
    strips = []
    size = D // (rings[0] * rings[1] * rings[2] * 2)
    for a in range(rings[0]):
        for b in range(rings[1]):
            for c in range(rings[2]):
                at = (a, b, c)
                order = ORDERS[color]
                place = 0
                for ring in order:
                    place = place * rings[ring] + at[ring]
                for core in range(2):
                    source = (((a * rings[1] + b) * rings[2] + c) * 2 + core) * size
                    strips.append((core, source, place * size))
    return size, strips


def locate(negative, spot, rings):
    per_device = 4
    owner = negative // per_device
    inner = negative % per_device
    y_size = rings[2]
    z_off = (owner // (2 * y_size) - spot[0] + rings[1]) % rings[1]
    y_off = ((owner // 2) % y_size - spot[1] + y_size) % y_size
    color = inner // 2
    near = jnp.where(color == 0, y_off, z_off)
    far = jnp.where(color == 0, z_off, y_off)
    half = jnp.where((near == 0) | (near == 3), 0, 1)
    row = inner % 2 + jnp.where((near == 2) | (near == 3), 2, 0)
    kind = jnp.where(far == 0, 0, jnp.where(far == 3, 1, jnp.where(far == 1, 2, 3)))
    other = (owner + spot[2]) % 2
    number = kind * 2 + half
    phase = jnp.where(kind == 3, 2, jnp.where((number == 3) | (number == 4), 1, 0))
    return (other * 2 + color) * 8 + number, row, phase


def negatives_kernel(
    pick_ref, tan_ref, spot_ref, text_ref, qx_ref, mhx_ref, ones_ref, kvw_ref, head_ref, dq_in_ref, lrow_in_ref,
    grad_in_ref, *rest,
    pairs, rings, blocks, phase,
):
    last = phase == 2
    pieces, rest = rest[: len(blocks)], rest[len(blocks) :]
    if last:
        mine_ref, other_ref, lrow_ref = rest[:3]
    else:
        out_grad_ref, out_dq_ref, lrow_ref = rest[:3]
    (
        kv_ref, dkv_ref, xt_ref, image_ref, grad_ref, prior_ref, dq_ref, out_ref, list_ref,
        sems, prior_sem, out_sems,
    ) = rest[3:]
    spot = [spot_ref[k] for k in range(3)]
    count = jnp.int32(0)
    for j in range(pairs):
        block, row, when = locate(pick_ref[j], spot, rings)
        here = when == phase
        list_ref[count] = j
        for k, piece in enumerate(pieces):

            @pl.when(here & (block == blocks[k]))
            def _():
                pltpu.make_async_copy(piece.at[row], image_ref.at[count], sems.at[count]).start()

        count = count + here.astype(jnp.int32)
    prior = pltpu.make_async_copy(grad_in_ref, prior_ref, prior_sem)
    prior.start()
    dq_ref[...] = dq_in_ref[...]
    lrow_ref[...] = lrow_in_ref[...]

    def one(i, carry):
        dkv_ref[pl.ds(pl.multiple_of(i * LX + LP - 8, 64), LX - LP + 8), :] = jnp.zeros((LX - LP + 8, 2 * D), BF16)
        pltpu.make_async_copy(pieces[0].at[0], image_ref.at[i], sems.at[i]).wait()
        j = list_ref[i]
        image = image_ref[i]
        kv_ref[...] = nn(image, kvw_ref[...]).astype(BF16)
        wide = jnp.concatenate([image, jnp.zeros((LX - LP, D), BF16)], axis=0)
        xt_ref[i] = wide.T
        attend_pair(
            i, j, j // 2, tan_ref[j], lambda lo: kv_ref[:, lo : lo + GW],
            qx_ref, head_ref, mhx_ref, ones_ref, dkv_ref, dq_ref, lrow_ref,
        )
        return carry

    lax.fori_loop(0, count, one, 0)
    twos = (count + 1) // 2

    @pl.when(count % 2 == 1)
    def _():
        dkv_ref[pl.ds(pl.multiple_of(count * LX, LX), LX), :] = jnp.zeros((LX, 2 * D), BF16)
        xt_ref[count] = jnp.zeros((D, LX), BF16)

    def products(part):
        def two(k, carry):
            left = xt_ref[2 * k]
            right = xt_ref[2 * k + 1]
            rows = pl.ds(pl.multiple_of(2 * k * LX, LX), LX)
            more = pl.ds(pl.multiple_of((2 * k + 1) * LX, LX), LX)

            def cols(n, inner):
                at = pl.ds(pl.multiple_of(n * GW, GW), GW)
                wide = pl.ds(pl.multiple_of(part * D + n * GW, GW), GW)
                prior_ref[:, wide] += nn(left, dkv_ref[rows, wide]) + nn(right, dkv_ref[more, wide])
                return inner

            return lax.fori_loop(0, D // GW, cols, carry)

        lax.fori_loop(0, twos, two, 0)

    if not last:
        prior.wait()
        products(0)
        products(1)
        out_grad_ref[...] = prior_ref[...]
        out_dq_ref[...] = dq_ref[...]
        return

    core = spot[2]
    half = D // 2

    def spread(color, source_ref, lo):
        size, strips = strip_rows(color, rings)
        for which, source, target in strips:
            slot = jnp.where(core == which, 0, 1)
            out_ref[slot, color * half + target : color * half + target + size, :] = source_ref[
                source : source + size, lo : lo + D
            ]
        copies = []
        for slot, ref in ((1, other_ref), (0, mine_ref)):
            copy = pltpu.make_async_copy(
                out_ref.at[slot, pl.ds(color * half, half)],
                ref.at[pl.ds(color * half, half)],
                out_sems.at[2 * color + slot],
            )
            copy.start()
            copies.append(copy)
        return copies

    grad_ref[...] = tn(text_ref[...], dq_ref[...].astype(BF16))
    copies = spread(0, grad_ref, 0)
    prior.wait()
    for part in range(2):
        products(part)
        copies += spread(part + 1, prior_ref, part * D)
    for copy in copies:
        copy.wait()


VM = pl.BlockSpec(memory_space=pltpu.VMEM)
SM = pl.BlockSpec(memory_space=pltpu.SMEM)
ANY = pl.BlockSpec(memory_space=pl.ANY)
LIMIT = 60 * 1024 * 1024


def own_pairs(tangent, text, query_weight, images, kv_weight, head):
    pairs = images.shape[0]
    return pl.pallas_call(
        functools.partial(own_kernel, pairs=pairs),
        name="own_pairs",
        in_specs=[SM] + [VM] * 5,
        out_specs=[VM] * 6,
        out_shape=[
            jax.ShapeDtypeStruct((pairs * GROUPS, ROWS, GW), BF16),
            jax.ShapeDtypeStruct((3 * GROUPS, ROWS, GW), BF16),
            jax.ShapeDtypeStruct((ROWS, GW), BF16),
            jax.ShapeDtypeStruct((D, 2 * D), F32),
            jax.ShapeDtypeStruct((pairs * QP, D), F32),
            jax.ShapeDtypeStruct((pairs, GW), F32),
        ],
        scratch_shapes=[
            pltpu.VMEM((LP, 2 * D), BF16),
            pltpu.VMEM((pairs * LX, 2 * D), BF16),
            pltpu.VMEM((D, pairs * LX), BF16),
        ],
        compiler_params=pltpu.CompilerParams(vmem_limit_bytes=LIMIT),
    )(tangent, text, query_weight, images, kv_weight, head)


def negative_pairs(picks, tangent, spot, text, made, kv_weight, head, dq, lrow, grad, arrived, rings, phase):
    last = phase == 2
    pairs = picks.shape[0]
    blocks = tuple(arrived)
    half = jax.ShapeDtypeStruct((3 * D // 2, D), F32)
    rows = jax.ShapeDtypeStruct(lrow.shape, F32)
    if last:
        out_shape, out_specs = [half, half, rows], [ANY, ANY, VM]
    else:
        out_shape = [jax.ShapeDtypeStruct(grad.shape, F32), jax.ShapeDtypeStruct(dq.shape, F32), rows]
        out_specs = [VM] * 3
    return pl.pallas_call(
        functools.partial(negatives_kernel, pairs=pairs, rings=rings, blocks=blocks, phase=phase),
        in_specs=[SM] * 3 + [VM] * 8 + [ANY] * (1 + len(blocks)),
        out_specs=out_specs,
        out_shape=out_shape,
        scratch_shapes=[
            pltpu.VMEM((LP, 2 * D), BF16),
            pltpu.VMEM((pairs * LX, 2 * D), BF16),
            pltpu.VMEM((pairs, D, LX), BF16),
            pltpu.VMEM((pairs, LP, D), BF16),
            pltpu.VMEM((D, D) if last else (8, 128), F32),
            pltpu.VMEM((D, 2 * D), F32),
            pltpu.VMEM(dq.shape, F32),
            pltpu.VMEM((2, 3 * D // 2, D) if last else (2, 8, 128), F32),
            pltpu.SMEM((pairs + 1,), jnp.int32),
            pltpu.SemaphoreType.DMA((pairs + 1,)),
            pltpu.SemaphoreType.DMA(()),
            pltpu.SemaphoreType.DMA((6,)),
        ],
        compiler_params=pltpu.CompilerParams(vmem_limit_bytes=LIMIT),
    )(picks, tangent, spot, text, *made, kv_weight, head, dq, lrow, grad, *arrived.values())


def shift(x, axis, step):
    n = lax.axis_size(axis)
    return lax.ppermute(x, axis, [(k, (k + step) % n) for k in range(n)])


AXES = (("dev_1", "dev_0"), ("dev_0", "dev_1"))


def first_steps(images):
    blocks = []
    for color, (near, _) in enumerate(AXES):
        own = images[2 * color : 2 * color + 2]
        blocks.append((own, shift(own, near, 1), shift(own, near, -1)))
    return blocks


def other_core(blocks):
    return blocks | {16 + k: shift(block, "dev_2", 1) for k, block in blocks.items()}


def next_steps(first):
    soon, then = {}, {}
    for color, (near, far) in enumerate(AXES):
        own, left, right = first[color]
        left_far, right_far = shift(left[:1], near, 1), shift(right[1:], near, -1)
        a = jnp.concatenate([own, left])
        b = jnp.concatenate([right, left_far, right_far])
        soon[color * 8] = a
        soon[color * 8 + 1] = b
        soon[color * 8 + 2] = shift(a, far, 1)
        soon[color * 8 + 5] = shift(b, far, -1)
        then[color * 8 + 3] = shift(b, far, 1)
        then[color * 8 + 4] = shift(a, far, -1)
    return soon, then


def last_steps(soon):
    blocks = {}
    for color, (_, far) in enumerate(AXES):
        blocks[color * 8 + 6] = shift(soon[color * 8 + 2], far, 1)
        blocks[color * 8 + 7] = shift(soon[color * 8 + 5], far, -1)
    return blocks


def together(blocks, other):
    keys = sorted(blocks)
    out = lax.optimization_barrier((other, *[blocks[k] for k in keys]))
    return dict(zip(keys, out[1:])), out[0]


def ring_scatter(blocks, axis):
    n = lax.axis_size(axis)
    me = lax.axis_index(axis)
    sent = []
    for step in range(1, n):
        piece = lax.dynamic_index_in_dim(blocks, (me + step) % n, 0, keepdims=False)
        sent.append(lax.ppermute(piece, axis, [(k, (k + step) % n) for k in range(n)]))
    return sent, lax.dynamic_index_in_dim(blocks, me, 0, keepdims=False)


def reduce_gradients(mine, other):
    from_core = lax.ppermute(other, "dev_2", [(0, 1), (1, 0)])
    half = mine.shape[0] // 3
    parts = [
        mine[k * half : (k + 1) * half] + from_core[k * half : (k + 1) * half] for k in range(3)
    ]
    width = mine.shape[1]
    for stage in range(3):
        moved = []
        for ring, axis in enumerate(RINGS):
            colors = [k for k in range(3) if ORDERS[k][stage] == ring]
            if not colors:
                continue
            n = lax.axis_size(axis)
            blocks = [parts[k].reshape(n, parts[k].shape[0] // n, width) for k in colors]
            rows = blocks[0].shape[1]
            moved.append((colors, rows, ring_scatter(jnp.concatenate(blocks, axis=1), axis)))
        for colors, rows, (sent, kept) in moved:
            for piece in sent:
                kept = kept + piece
            for place, k in enumerate(colors):
                parts[k] = kept[place * rows : (place + 1) * rows]
    return parts


def local(image_tokens, text_tokens, negatives, query_weight, kv_weight, match_head, cotangent):
    pairs, text_len, model = text_tokens.shape
    images = jnp.pad(image_tokens, ((0, 0), (0, LP - LI), (0, 0)))
    first = first_steps(images)
    text = jnp.pad(text_tokens, ((0, 0), (0, QP - LT), (0, 0))).reshape(pairs * QP, model)
    scale = cotangent.astype(F32) / text_len
    head = match_head.reshape(1, model)
    *made, grad, dq, own_rows = own_pairs(scale[:, 0], text, query_weight, images, kv_weight, head)
    soon, then = next_steps(first)
    passed, dq = together({k: v for k, v in soon.items() if k % 8 in (2, 5)}, dq)
    soon |= passed
    far_blocks = last_steps(soon)
    spot = jnp.stack([lax.axis_index(axis) for axis in DEV]).astype(jnp.int32)
    rings = tuple(lax.axis_size(ring) for ring in RINGS)
    picks = negatives.reshape(-1)
    far_scale = scale[:, 1:].reshape(-1)
    rows = jnp.zeros((picks.shape[0], GW), F32)
    grad, dq, rows = negative_pairs(
        picks, far_scale, spot, text, made, kv_weight, head, dq, rows, grad, other_core(soon), rings, 0
    )
    then, dq = together(then, dq)
    grad, dq, rows = negative_pairs(
        picks, far_scale, spot, text, made, kv_weight, head, dq, rows, grad, other_core(then), rings, 1
    )
    far_blocks, dq = together(far_blocks, dq)
    mine, other, rows = negative_pairs(
        picks, far_scale, spot, text, made, kv_weight, head, dq, rows, grad, other_core(far_blocks), rings, 2
    )
    own_logits = jnp.sum(own_rows, axis=1, keepdims=True)
    far_logits = jnp.sum(rows, axis=1).reshape(pairs, 2)
    logits = jnp.concatenate([own_logits, far_logits], axis=1) / text_len
    grad_query, grad_key, grad_value = reduce_gradients(mine, other)
    return logits, grad_query, jnp.concatenate([grad_key, grad_value], axis=1)


def solution(mesh):
    torus = Mesh(
        mesh.devices.reshape(mesh.shape["grp"], 4, 4, 2), ("grp", "dev_0", "dev_1", "dev_2")
    )
    placed = (
        P(GRP_DEV, None, None),
        P(GRP_DEV, None, None),
        P(GRP_DEV, None),
        P(),
        P(),
        P(),
        P(GRP_DEV, None),
    )
    return jax.shard_map(
        local,
        mesh=torus,
        in_specs=placed,
        out_specs=(P(GRP_DEV, None), P(GRP_DEV, None), P(GRP_DEV, None)),
        check_vma=False,
    )
```

profile of v0, /device:TPU:0, one launch (start us, length us, event | category | flops | bytes accessed | tf_op | source)
XLA Modules:
  0.0 264.3 jit_solution(7577237478443450461)
XLA Ops:
  2.1 1.8 collective-permute-start
  3.9 1.9 collective-permute-start.6
  5.8 2.1 collective-permute-start.8
  7.9 1.7 collective-permute-start.2
  9.6 9.6 %collective-permute-done = bf16[2,200,768]{2,1,0:T(8,128)(2,1)S(1)} collective-permute-done((bf16[2,200,768]{2,1,0:T(8,128)(2,1)S(1)}, bf16[2,200,768]{2,1,0:T(8,128)(2,1)S(1)}, u32[]{:S(2)}, u32[]{:S(2)}) %collective-permute-start) | collective-permute-done | bytes 614432 | tf_op jit(solution)/shard_map/ppermute | solution.py:347
  19.3 2.0 collective-permute-start.1
  21.5 1.8 collective-permute-start.9
  23.3 1.6 collective-permute-start.10
  24.9 1.6 collective-permute-start.3
  26.6 1.7 collective-permute-start.4
  30.3 25.9 %collective-permute-done.9 = bf16[1,200,768]{2,1,0:T(8,128)(2,1)S(1)} collective-permute-done((bf16[1,200,768]{2,1,0:T(8,128)(2,1)S(1)}, bf16[1,200,768]{2,1,0:T(8,128)(2,1)S(1)}, u32[]{:S(2)}, u32[]{:S(2)}) %collective-permute-start.9) | collective-permute-done | bytes 307232 | tf_op jit(solution)/shard_map/ppermute | solution.py:347
  58.0 3.0 %collective-permute-start.11 = (bf16[4,200,768]{2,1,0:T(8,128)(2,1)}, bf16[4,200,768]{2,1,0:T(8,128)(2,1)}, u32[]{:S(2)}, u32[]{:S(2)}) collective-permute-start(bf16[4,200,768]{2,1,0:T(8,128)(2,1)} %constant_dynamic-update-slice_fusion.3.rest_5_), channel_id=1, source_target_pairs={{0,6},{2,0},{4,2},{6,4},{1,7},{3,1},{5,3},{7,5},{8,14},{10,8},{12,... | collective-permute-start | bytes 3686408 | tf_op jit(solution)/shard_map/ppermute | solution.py:347
  62.4 1.7 collective-permute-start.5
  67.8 16.6 %own_pairs.1 = (bf16[12,128,256]{2,1,0:T(8,128)(2,1)}, bf16[9,128,256]{2,1,0:T(8,128)(2,1)}, bf16[128,256]{1,0:T(8,128)(2,1)}, f32[768,1536]{1,0:T(8,128)}, f32[128,768]{1,0:T(8,128)}, /*index=5*/f32[4,256]{1,0:T(4,128)}) custom-call(f32[4]{0:T(128)} %slice_reduce_fusion.tan_ref, bf16[128,768]{1,0:T(8,128)(2,1)} %bitcast.99, bf16[768,768]{1,0:T(8,128)(2,1)} %qw_ref.1, ...), custom_call_target="tpu_custom_call" | custom-call | tf_op jit(solution)/shard_map/own_pairs/pallas_call | solution.py:289
  85.9 3.7 %collective-permute-done.5.rest_3_ = bf16[4,200,768]{2,1,0:T(8,128)(2,1)} collective-permute-done((bf16[4,200,768]{2,1,0:T(8,128)(2,1)}, bf16[4,200,768]{2,1,0:T(8,128)(2,1)}, u32[]{:S(2)}, u32[]{:S(2)}) %collective-permute-start.5) | collective-permute-done | bytes 1228832 | tf_op jit(solution)/shard_map/ppermute | solution.py:347
  90.6 2.7 %collective-permute-start.21 = (bf16[4,200,768]{2,1,0:T(8,128)(2,1)S(1)}, bf16[4,200,768]{2,1,0:T(8,128)(2,1)}, u32[]{:S(2)}, u32[]{:S(2)}) collective-permute-start(bf16[4,200,768]{2,1,0:T(8,128)(2,1)S(1)} %pad_maximum_fusion.rest_0_), channel_id=1, source_target_pairs={{0,24},{8,0},{16,8},{24,16},{1,25},{9,1},{17,9},{25,17},{2,26},{10... | collective-permute-start | bytes 3686408 | tf_op jit(solution)/shard_map/ppermute | solution.py:347
  100.0 16.4 %shard_map.94 = (f32[768,1536]{1,0:T(8,128)}, f32[128,768]{1,0:T(8,128)}, f32[8,256]{1,0:T(8,128)}) custom-call(s32[8]{0:T(128)} %reshape.50.pick_ref, f32[8]{0:T(128)} %reshape.51.tan_ref, s32[3]{0:T(128)} %pad_add_fusion.spot_ref, bf16[128,768]{1,0:T(8,128)(2,1)} %bitcast.100, bf16[12,128,256]{2,1,0:T(8,128)(2,1)} %get-tuple-element.34.qx_ref, ...), custom_call_target="tpu_custom_call" | custom-call | tf_op jit(solution)/shard_map/pallas_call | solution.py:322
  116.4 3.5 %collective-permute-done.21.rest_1_ = bf16[4,200,768]{2,1,0:T(8,128)(2,1)} collective-permute-done((bf16[4,200,768]{2,1,0:T(8,128)(2,1)S(1)}, bf16[4,200,768]{2,1,0:T(8,128)(2,1)}, u32[]{:S(2)}, u32[]{:S(2)}) %collective-permute-start.21) | collective-permute-done | bytes 1228832 | tf_op jit(solution)/shard_map/ppermute | solution.py:347
  119.9 2.4 collective-permute-done.23.rest_3_
  122.3 2.8 %collective-permute-done.20.rest_0_ = bf16[4,200,768]{2,1,0:T(8,128)(2,1)} collective-permute-done((bf16[4,200,768]{2,1,0:T(8,128)(2,1)}, bf16[4,200,768]{2,1,0:T(8,128)(2,1)}, u32[]{:S(2)}, u32[]{:S(2)}) %collective-permute-start.20) | collective-permute-done | bytes 1228832 | tf_op jit(solution)/shard_map/ppermute | solution.py:347
  125.1 1.8 collective-permute-done.22.rest_2_
  127.8 2.1 collective-permute-done.24.rest_4_
  130.0 2.7 %collective-permute-start.29 = (bf16[4,200,768]{2,1,0:T(8,128)(2,1)}, bf16[4,200,768]{2,1,0:T(8,128)(2,1)S(1)}, u32[]{:S(2)}, u32[]{:S(2)}) collective-permute-start(bf16[4,200,768]{2,1,0:T(8,128)(2,1)} %collective-permute-done.5.rest_3_), channel_id=1, source_target_pairs={{0,24},{8,0},{16,8},{24,16},{1,25},{9,1},{17,9},{25,17},{2,26},{10... | collective-permute-start | bytes 3686408 | tf_op jit(solution)/shard_map/ppermute | solution.py:347
  133.7 3.2 %collective-permute-start.31 = (bf16[4,200,768]{2,1,0:T(8,128)(2,1)}, bf16[4,200,768]{2,1,0:T(8,128)(2,1)}, u32[]{:S(2)}, u32[]{:S(2)}) collective-permute-start(bf16[4,200,768]{2,1,0:T(8,128)(2,1)} %collective-permute-done.11.rest_7_), channel_id=1, source_target_pairs={{0,6},{2,0},{4,2},{6,4},{1,7},{3,1},{5,3},{7,5},{8,14},{10,8},{12,... | collective-permute-start | bytes 3686408 | tf_op jit(solution)/shard_map/ppermute | solution.py:347
  136.9 16.5 %shard_map.95 = (f32[768,1536]{1,0:T(8,128)}, f32[128,768]{1,0:T(8,128)}, f32[8,256]{1,0:T(8,128)}) custom-call(s32[8]{0:T(128)} %reshape.50.pick_ref, f32[8]{0:T(128)} %reshape.51.tan_ref, s32[3]{0:T(128)} %pad_add_fusion.spot_ref, bf16[128,768]{1,0:T(8,128)(2,1)} %bitcast.101, bf16[12,128,256]{2,1,0:T(8,128)(2,1)} %get-tuple-element.34.qx_ref, ...), custom_call_target="tpu_custom_call" | custom-call | tf_op jit(solution)/shard_map/pallas_call | solution.py:322
  153.5 4.7 %collective-permute-done.28.rest_0_ = bf16[4,200,768]{2,1,0:T(8,128)(2,1)S(1)} collective-permute-done((bf16[4,200,768]{2,1,0:T(8,128)(2,1)}, bf16[4,200,768]{2,1,0:T(8,128)(2,1)S(1)}, u32[]{:S(2)}, u32[]{:S(2)}) %collective-permute-start.28) | collective-permute-done | bytes 1228832 | tf_op jit(solution)/shard_map/ppermute | solution.py:347
  159.5 4.4 %collective-permute-done.30.rest_2_ = bf16[4,200,768]{2,1,0:T(8,128)(2,1)S(1)} collective-permute-done((bf16[4,200,768]{2,1,0:T(8,128)(2,1)}, bf16[4,200,768]{2,1,0:T(8,128)(2,1)S(1)}, u32[]{:S(2)}, u32[]{:S(2)}) %collective-permute-start.30) | collective-permute-done | bytes 1228832 | tf_op jit(solution)/shard_map/ppermute | solution.py:347
  164.9 1.9 collective-permute-done.32.rest_4_
  166.8 1.8 collective-permute-done.33.rest_5_
  168.6 1.8 collective-permute-done.34.rest_6_
  170.3 1.8 collective-permute-done.35.rest_7_
  173.2 13.4 %shard_map.96 = (f32[1152,768]{1,0:T(8,128)}, f32[1152,768]{1,0:T(8,128)}, f32[8,256]{1,0:T(8,128)}) custom-call(s32[8]{0:T(128)} %reshape.50.pick_ref, f32[8]{0:T(128)} %reshape.51.tan_ref, s32[3]{0:T(128)} %pad_add_fusion.spot_ref, bf16[128,768]{1,0:T(8,128)(2,1)} %bitcast.102, bf16[12,128,256]{2,1,0:T(8,128)(2,1)} %get-tuple-element.34.qx_ref, ...), custom_call_target="tpu_custom_call" | custom-call | tf_op jit(solution)/shard_map/pallas_call | solution.py:322
  187.9 5.2 %collective-permute-done.36 = f32[1152,768]{1,0:T(8,128)S(1)} collective-permute-done((f32[1152,768]{1,0:T(8,128)}, f32[1152,768]{1,0:T(8,128)S(1)}, u32[]{:S(2)}, u32[]{:S(2)}) %collective-permute-start.36) | collective-permute-done | bytes 3538976 | tf_op jit(solution)/shard_map/ppermute | solution.py:406
  193.1 2.4 slice_add_fusion
  195.7 7.8 %collective-permute-start.50 = (f32[96,768]{1,0:T(8,128)S(1)}, f32[96,768]{1,0:T(8,128)S(1)}, u32[]{:S(2)}, u32[]{:S(2)}) collective-permute-start(f32[96,768]{1,0:T(8,128)S(1)} %get-tuple-element.70), channel_id=1, source_target_pairs={{0,4},{2,6},{4,0},{6,2},{1,5},{3,7},{5,1},{7,3},{8,12},{10,14},{12... | collective-permute-start | bytes 884744 | tf_op jit(solution)/shard_map/ppermute | solution.py:401
  203.5 2.5 collective-permute-start.51
  206.8 4.0 %collective-permute-start.41 = (f32[96,768]{1,0:T(8,128)S(1)}, f32[96,768]{1,0:T(8,128)S(1)}, u32[]{:S(2)}, u32[]{:S(2)}) collective-permute-start(f32[96,768]{1,0:T(8,128)S(1)} %get-tuple-element.73), channel_id=1, source_target_pairs={{0,16},{8,24},{16,0},{24,8},{1,17},{9,25},{17,1},{25,9},{2,18},{10... | collective-permute-start | bytes 884744 | tf_op jit(solution)/shard_map/ppermute | solution.py:401
  210.9 3.5 %collective-permute-start.42 = (f32[96,768]{1,0:T(8,128)S(1)}, f32[96,768]{1,0:T(8,128)S(1)}, u32[]{:S(2)}, u32[]{:S(2)}) collective-permute-start(f32[96,768]{1,0:T(8,128)S(1)} %get-tuple-element.72), channel_id=1, source_target_pairs={{0,24},{8,0},{16,8},{24,16},{1,25},{9,1},{17,9},{25,17},{2,26},{10... | collective-permute-start | bytes 884744 | tf_op jit(solution)/shard_map/ppermute | solution.py:401
  214.5 2.6 collective-permute-done.50
  217.0 4.2 %collective-permute-start.37 = (f32[96,768]{1,0:T(8,128)S(1)}, f32[96,768]{1,0:T(8,128)S(1)}, u32[]{:S(2)}, u32[]{:S(2)}) collective-permute-start(f32[96,768]{1,0:T(8,128)S(1)} %get-tuple-element.74), channel_id=1, source_target_pairs={{0,32},{32,64},{64,96},{96,0},{1,33},{33,65},{65,97},{97,1},{2,34}... | collective-permute-start | bytes 884744 | tf_op jit(solution)/shard_map/ppermute | solution.py:401
  221.2 3.5 %collective-permute-start.38 = (f32[96,768]{1,0:T(8,128)S(1)}, f32[96,768]{1,0:T(8,128)S(1)}, u32[]{:S(2)}, u32[]{:S(2)}) collective-permute-start(f32[96,768]{1,0:T(8,128)S(1)} %get-tuple-element.76), channel_id=1, source_target_pairs={{0,64},{32,96},{64,0},{96,32},{1,65},{33,97},{65,1},{97,33},{2,66}... | collective-permute-start | bytes 884744 | tf_op jit(solution)/shard_map/ppermute | solution.py:401
  225.4 8.2 %collective-permute-start.53 = (f32[24,768]{1,0:T(8,128)S(1)}, f32[24,768]{1,0:T(8,128)S(1)}, u32[]{:S(2)}, u32[]{:S(2)}) collective-permute-start(f32[24,768]{1,0:T(8,128)S(1)} %get-tuple-element.82), channel_id=1, source_target_pairs={{0,16},{8,24},{16,0},{24,8},{1,17},{9,25},{17,1},{25,9},{2,18},{10... | collective-permute-start | bytes 221192 | tf_op jit(solution)/shard_map/ppermute | solution.py:401
  234.4 2.7 %collective-permute-done.38 = f32[96,768]{1,0:T(8,128)S(1)} collective-permute-done((f32[96,768]{1,0:T(8,128)S(1)}, f32[96,768]{1,0:T(8,128)S(1)}, u32[]{:S(2)}, u32[]{:S(2)}) %collective-permute-start.38) | collective-permute-done | bytes 294944 | tf_op jit(solution)/shard_map/ppermute | solution.py:401
  238.7 2.5 collective-permute-start.45
  241.3 4.6 %collective-permute-done.43 = f32[48,768]{1,0:T(8,128)S(1)} collective-permute-done((f32[48,768]{1,0:T(8,128)S(1)}, f32[48,768]{1,0:T(8,128)S(1)}, u32[]{:S(2)}, u32[]{:S(2)}) %collective-permute-start.43) | collective-permute-done | bytes 147488 | tf_op jit(solution)/shard_map/ppermute | solution.py:401
  246.8 6.7 %collective-permute-start.47 = (f32[6,768]{1,0:T(8,128)S(1)}, f32[6,768]{1,0:T(8,128)S(1)}, u32[]{:S(2)}, u32[]{:S(2)}) collective-permute-start(f32[6,768]{1,0:T(8,128)S(1)} %get-tuple-element.90), channel_id=1, source_target_pairs={{0,16},{8,24},{16,0},{24,8},{1,17},{9,25},{17,1},{25,9},{2,18},{10... | collective-permute-start | bytes 55304 | tf_op jit(solution)/shard_map/ppermute | solution.py:401
  256.1 3.4 %collective-permute-start.56 = (f32[12,768]{1,0:T(8,128)S(1)}, f32[12,768]{1,0:T(8,128)S(1)}, u32[]{:S(2)}, u32[]{:S(2)}) collective-permute-start(f32[12,768]{1,0:T(8,128)S(1)} %get-tuple-element.84), channel_id=1, source_target_pairs={{0,64},{32,96},{64,0},{96,32},{1,65},{33,97},{65,1},{97,33},{2,66}... | collective-permute-start | bytes 110600 | tf_op jit(solution)/shard_map/ppermute | solution.py:401
  262.1 1.5 collective-permute-done.57
  (168 shorter events, 37.3 us)
Async XLA Ops:
  2.1 17.0 %collective-permute-start = (bf16[2,200,768]{2,1,0:T(8,128)(2,1)S(1)}, bf16[2,200,768]{2,1,0:T(8,128)(2,1)S(1)}, u32[]{:S(2)}, u32[]{:S(2)}) collective-permute-start(bf16[2,200,768]{2,1,0:T(8,128)(2,1)S(1)} %get-tuple-element.67), channel_id=1, source_target_pairs={{0,2},{2,4},{4,6},{6,0},{1,3},{3,5},{5,7},{7,1},{8,10},{10,12},{12... | collective-permute-start | bytes 1843208 | tf_op jit(solution)/shard_map/ppermute | solution.py:347
  3.9 17.6 %collective-permute-start.6 = (bf16[2,200,768]{2,1,0:T(8,128)(2,1)S(1)}, bf16[2,200,768]{2,1,0:T(8,128)(2,1)S(1)}, u32[]{:S(2)}, u32[]{:S(2)}) collective-permute-start(bf16[2,200,768]{2,1,0:T(8,128)(2,1)S(1)} %get-tuple-element.66), channel_id=1, source_target_pairs={{0,8},{8,16},{16,24},{24,0},{1,9},{9,17},{17,25},{25,1},{2,10},{10... | collective-permute-start | bytes 1843208 | tf_op jit(solution)/shard_map/ppermute | solution.py:347
  5.8 17.5 %collective-permute-start.8 = (bf16[2,200,768]{2,1,0:T(8,128)(2,1)S(1)}, bf16[2,200,768]{2,1,0:T(8,128)(2,1)S(1)}, u32[]{:S(2)}, u32[]{:S(2)}) collective-permute-start(bf16[2,200,768]{2,1,0:T(8,128)(2,1)S(1)} %get-tuple-element.66), channel_id=1, source_target_pairs={{0,24},{8,0},{16,8},{24,16},{1,25},{9,1},{17,9},{25,17},{2,26},{10... | collective-permute-start | bytes 1843208 | tf_op jit(solution)/shard_map/ppermute | solution.py:347
  7.9 18.7 %collective-permute-start.2 = (bf16[2,200,768]{2,1,0:T(8,128)(2,1)S(1)}, bf16[2,200,768]{2,1,0:T(8,128)(2,1)S(1)}, u32[]{:S(2)}, u32[]{:S(2)}) collective-permute-start(bf16[2,200,768]{2,1,0:T(8,128)(2,1)S(1)} %get-tuple-element.67), channel_id=1, source_target_pairs={{0,6},{2,0},{4,2},{6,4},{1,7},{3,1},{5,3},{7,5},{8,14},{10,8},{12,... | collective-permute-start | bytes 1843208 | tf_op jit(solution)/shard_map/ppermute | solution.py:347
  19.3 44.9 %collective-permute-start.1 = (bf16[4,200,768]{2,1,0:T(8,128)(2,1)S(1)}, bf16[4,200,768]{2,1,0:T(8,128)(2,1)S(1)}, u32[]{:S(2)}, u32[]{:S(2)}) collective-permute-start(bf16[4,200,768]{2,1,0:T(8,128)(2,1)S(1)} %pad_maximum_fusion.rest_0_), channel_id=1, source_target_pairs={{0,8},{8,16},{16,24},{24,0},{1,9},{9,17},{17,25},{25,1},{2,10},{10... | collective-permute-start | bytes 3686408 | tf_op jit(solution)/shard_map/ppermute | solution.py:347
  21.5 34.7 %collective-permute-start.9 = (bf16[1,200,768]{2,1,0:T(8,128)(2,1)S(1)}, bf16[1,200,768]{2,1,0:T(8,128)(2,1)S(1)}, u32[]{:S(2)}, u32[]{:S(2)}) collective-permute-start(bf16[1,200,768]{2,1,0:T(8,128)(2,1)S(1)} %slice.74), channel_id=1, source_target_pairs={{0,8},{8,16},{16,24},{24,0},{1,9},{9,17},{17,25},{25,1},{2,10},{10... | collective-permute-start | bytes 921608 | tf_op jit(solution)/shard_map/ppermute | solution.py:347
  23.3 33.9 %collective-permute-start.10 = (bf16[1,200,768]{2,1,0:T(8,128)(2,1)S(1)}, bf16[1,200,768]{2,1,0:T(8,128)(2,1)S(1)}, u32[]{:S(2)}, u32[]{:S(2)}) collective-permute-start(bf16[1,200,768]{2,1,0:T(8,128)(2,1)S(1)} %slice.75), channel_id=1, source_target_pairs={{0,24},{8,0},{16,8},{24,16},{1,25},{9,1},{17,9},{25,17},{2,26},{10... | collective-permute-start | bytes 921608 | tf_op jit(solution)/shard_map/ppermute | solution.py:347
  24.9 36.0 %collective-permute-start.3 = (bf16[1,200,768]{2,1,0:T(8,128)(2,1)S(1)}, bf16[1,200,768]{2,1,0:T(8,128)(2,1)S(1)}, u32[]{:S(2)}, u32[]{:S(2)}) collective-permute-start(bf16[1,200,768]{2,1,0:T(8,128)(2,1)S(1)} %slice.72), channel_id=1, source_target_pairs={{0,2},{2,4},{4,6},{6,0},{1,3},{3,5},{5,7},{7,1},{8,10},{10,12},{12... | collective-permute-start | bytes 921608 | tf_op jit(solution)/shard_map/ppermute | solution.py:347
  26.6 35.1 %collective-permute-start.4 = (bf16[1,200,768]{2,1,0:T(8,128)(2,1)S(1)}, bf16[1,200,768]{2,1,0:T(8,128)(2,1)S(1)}, u32[]{:S(2)}, u32[]{:S(2)}) collective-permute-start(bf16[1,200,768]{2,1,0:T(8,128)(2,1)S(1)} %slice.73), channel_id=1, source_target_pairs={{0,6},{2,0},{4,2},{6,4},{1,7},{3,1},{5,3},{7,5},{8,14},{10,8},{12,... | collective-permute-start | bytes 921608 | tf_op jit(solution)/shard_map/ppermute | solution.py:347
  56.2 28.7 %collective-permute-start.7 = (bf16[4,200,768]{2,1,0:T(8,128)(2,1)S(1)}, bf16[4,200,768]{2,1,0:T(8,128)(2,1)}, u32[]{:S(2)}, u32[]{:S(2)}) collective-permute-start(bf16[4,200,768]{2,1,0:T(8,128)(2,1)S(1)} %pad_maximum_fusion.1.rest_4_), channel_id=1, source_target_pairs={{0,2},{2,4},{4,6},{6,0},{1,3},{3,5},{5,7},{7,1},{8,10},{10,12},{12... | collective-permute-start | bytes 3686408 | tf_op jit(solution)/shard_map/ppermute | solution.py:347
  58.0 27.9 %collective-permute-start.11 = (bf16[4,200,768]{2,1,0:T(8,128)(2,1)}, bf16[4,200,768]{2,1,0:T(8,128)(2,1)}, u32[]{:S(2)}, u32[]{:S(2)}) collective-permute-start(bf16[4,200,768]{2,1,0:T(8,128)(2,1)} %constant_dynamic-update-slice_fusion.3.rest_5_), channel_id=1, source_target_pairs={{0,6},{2,0},{4,2},{6,4},{1,7},{3,1},{5,3},{7,5},{8,14},{10,8},{12,... | collective-permute-start | bytes 3686408 | tf_op jit(solution)/shard_map/ppermute | solution.py:347
  62.4 27.1 %collective-permute-start.5 = (bf16[4,200,768]{2,1,0:T(8,128)(2,1)}, bf16[4,200,768]{2,1,0:T(8,128)(2,1)}, u32[]{:S(2)}, u32[]{:S(2)}) collective-permute-start(bf16[4,200,768]{2,1,0:T(8,128)(2,1)} %constant_dynamic-update-slice_fusion.rest_1_), channel_id=1, source_target_pairs={{0,24},{8,0},{16,8},{24,16},{1,25},{9,1},{17,9},{25,17},{2,26},{10... | collective-permute-start | bytes 3686408 | tf_op jit(solution)/shard_map/ppermute | solution.py:347
  64.2 25.4 %collective-permute-start.12 = (bf16[4,200,768]{2,1,0:T(8,128)(2,1)S(1)}, bf16[4,200,768]{2,1,0:T(8,128)(2,1)}, u32[]{:S(2)}, u32[]{:S(2)}) collective-permute-start(bf16[4,200,768]{2,1,0:T(8,128)(2,1)S(1)} %pad_maximum_fusion.rest_0_), channel_id=1, source_target_pairs={{0,1},{1,0},{2,3},{3,2},{4,5},{5,4},{6,7},{7,6},{8,9},{9,8},{10,11... | collective-permute-start | bytes 3686408 | tf_op jit(solution)/shard_map/ppermute | solution.py:347
  64.2 25.9 %collective-permute-start.16 = (bf16[4,200,768]{2,1,0:T(8,128)(2,1)S(1)}, bf16[4,200,768]{2,1,0:T(8,128)(2,1)}, u32[]{:S(2)}, u32[]{:S(2)}) collective-permute-start(bf16[4,200,768]{2,1,0:T(8,128)(2,1)S(1)} %pad_maximum_fusion.1.rest_4_), channel_id=1, source_target_pairs={{0,1},{1,0},{2,3},{3,2},{4,5},{5,4},{6,7},{7,6},{8,9},{9,8},{10,11... | collective-permute-start | bytes 3686408 | tf_op jit(solution)/shard_map/ppermute | solution.py:347
  90.1 6.1 %collective-permute-start.18 = (bf16[4,200,768]{2,1,0:T(8,128)(2,1)}, bf16[4,200,768]{2,1,0:T(8,128)(2,1)S(1)}, u32[]{:S(2)}, u32[]{:S(2)}) collective-permute-start(bf16[4,200,768]{2,1,0:T(8,128)(2,1)} %collective-permute-done.7.rest_6_), channel_id=1, source_target_pairs={{0,1},{1,0},{2,3},{3,2},{4,5},{5,4},{6,7},{7,6},{8,9},{9,8},{10,11... | collective-permute-start | bytes 3686408 | tf_op jit(solution)/shard_map/ppermute | solution.py:347
  90.2 9.2 %collective-permute-start.19 = (bf16[4,200,768]{2,1,0:T(8,128)(2,1)}, bf16[4,200,768]{2,1,0:T(8,128)(2,1)}, u32[]{:S(2)}, u32[]{:S(2)}) collective-permute-start(bf16[4,200,768]{2,1,0:T(8,128)(2,1)} %collective-permute-done.11.rest_7_), channel_id=1, source_target_pairs={{0,1},{1,0},{2,3},{3,2},{4,5},{5,4},{6,7},{7,6},{8,9},{9,8},{10,11... | collective-permute-start | bytes 3686408 | tf_op jit(solution)/shard_map/ppermute | solution.py:347
  90.6 29.3 %collective-permute-start.21 = (bf16[4,200,768]{2,1,0:T(8,128)(2,1)S(1)}, bf16[4,200,768]{2,1,0:T(8,128)(2,1)}, u32[]{:S(2)}, u32[]{:S(2)}) collective-permute-start(bf16[4,200,768]{2,1,0:T(8,128)(2,1)S(1)} %pad_maximum_fusion.rest_0_), channel_id=1, source_target_pairs={{0,24},{8,0},{16,8},{24,16},{1,25},{9,1},{17,9},{25,17},{2,26},{10... | collective-permute-start | bytes 3686408 | tf_op jit(solution)/shard_map/ppermute | solution.py:347
  93.4 28.9 %collective-permute-start.23 = (bf16[4,200,768]{2,1,0:T(8,128)(2,1)S(1)}, bf16[4,200,768]{2,1,0:T(8,128)(2,1)}, u32[]{:S(2)}, u32[]{:S(2)}) collective-permute-start(bf16[4,200,768]{2,1,0:T(8,128)(2,1)S(1)} %pad_maximum_fusion.1.rest_4_), channel_id=1, source_target_pairs={{0,6},{2,0},{4,2},{6,4},{1,7},{3,1},{5,3},{7,5},{8,14},{10,8},{12,... | collective-permute-start | bytes 3686408 | tf_op jit(solution)/shard_map/ppermute | solution.py:347
  94.5 30.6 %collective-permute-start.20 = (bf16[4,200,768]{2,1,0:T(8,128)(2,1)}, bf16[4,200,768]{2,1,0:T(8,128)(2,1)}, u32[]{:S(2)}, u32[]{:S(2)}) collective-permute-start(bf16[4,200,768]{2,1,0:T(8,128)(2,1)} %constant_dynamic-update-slice_fusion.rest_1_), channel_id=1, source_target_pairs={{0,8},{8,16},{16,24},{24,0},{1,9},{9,17},{17,25},{25,1},{2,10},{10... | collective-permute-start | bytes 3686408 | tf_op jit(solution)/shard_map/ppermute | solution.py:347
  96.2 30.6 %collective-permute-start.22 = (bf16[4,200,768]{2,1,0:T(8,128)(2,1)}, bf16[4,200,768]{2,1,0:T(8,128)(2,1)}, u32[]{:S(2)}, u32[]{:S(2)}) collective-permute-start(bf16[4,200,768]{2,1,0:T(8,128)(2,1)} %constant_dynamic-update-slice_fusion.3.rest_5_), channel_id=1, source_target_pairs={{0,2},{2,4},{4,6},{6,0},{1,3},{3,5},{5,7},{7,1},{8,10},{10,12},{12... | collective-permute-start | bytes 3686408 | tf_op jit(solution)/shard_map/ppermute | solution.py:347
  127.3 6.4 %collective-permute-start.26 = (bf16[4,200,768]{2,1,0:T(8,128)(2,1)}, bf16[4,200,768]{2,1,0:T(8,128)(2,1)}, u32[]{:S(2)}, u32[]{:S(2)}) collective-permute-start(bf16[4,200,768]{2,1,0:T(8,128)(2,1)} %collective-permute-done.22.rest_2_), channel_id=1, source_target_pairs={{0,1},{1,0},{2,3},{3,2},{4,5},{5,4},{6,7},{7,6},{8,9},{9,8},{10,11... | collective-permute-start | bytes 3686408 | tf_op jit(solution)/shard_map/ppermute | solution.py:347
  127.3 9.6 %collective-permute-start.27 = (bf16[4,200,768]{2,1,0:T(8,128)(2,1)}, bf16[4,200,768]{2,1,0:T(8,128)(2,1)}, u32[]{:S(2)}, u32[]{:S(2)}) collective-permute-start(bf16[4,200,768]{2,1,0:T(8,128)(2,1)} %collective-permute-done.23.rest_3_), channel_id=1, source_target_pairs={{0,1},{1,0},{2,3},{3,2},{4,5},{5,4},{6,7},{7,6},{8,9},{9,8},{10,11... | collective-permute-start | bytes 3686408 | tf_op jit(solution)/shard_map/ppermute | solution.py:347
  127.8 30.4 %collective-permute-start.28 = (bf16[4,200,768]{2,1,0:T(8,128)(2,1)}, bf16[4,200,768]{2,1,0:T(8,128)(2,1)S(1)}, u32[]{:S(2)}, u32[]{:S(2)}) collective-permute-start(bf16[4,200,768]{2,1,0:T(8,128)(2,1)} %copy-done.2), channel_id=1, source_target_pairs={{0,8},{8,16},{16,24},{24,0},{1,9},{9,17},{17,25},{25,1},{2,10},{10... | collective-permute-start | bytes 3686408 | tf_op jit(solution)/shard_map/ppermute | solution.py:347
  130.0 29.6 %collective-permute-start.29 = (bf16[4,200,768]{2,1,0:T(8,128)(2,1)}, bf16[4,200,768]{2,1,0:T(8,128)(2,1)S(1)}, u32[]{:S(2)}, u32[]{:S(2)}) collective-permute-start(bf16[4,200,768]{2,1,0:T(8,128)(2,1)} %collective-permute-done.5.rest_3_), channel_id=1, source_target_pairs={{0,24},{8,0},{16,8},{24,16},{1,25},{9,1},{17,9},{25,17},{2,26},{10... | collective-permute-start | bytes 3686408 | tf_op jit(solution)/shard_map/ppermute | solution.py:347
  133.7 30.2 %collective-permute-start.30 = (bf16[4,200,768]{2,1,0:T(8,128)(2,1)}, bf16[4,200,768]{2,1,0:T(8,128)(2,1)S(1)}, u32[]{:S(2)}, u32[]{:S(2)}) collective-permute-start(bf16[4,200,768]{2,1,0:T(8,128)(2,1)} %collective-permute-done.7.rest_6_), channel_id=1, source_target_pairs={{0,2},{2,4},{4,6},{6,0},{1,3},{3,5},{5,7},{7,1},{8,10},{10,12},{12... | collective-permute-start | bytes 3686408 | tf_op jit(solution)/shard_map/ppermute | solution.py:347
  133.7 30.2 %collective-permute-start.31 = (bf16[4,200,768]{2,1,0:T(8,128)(2,1)}, bf16[4,200,768]{2,1,0:T(8,128)(2,1)}, u32[]{:S(2)}, u32[]{:S(2)}) collective-permute-start(bf16[4,200,768]{2,1,0:T(8,128)(2,1)} %collective-permute-done.11.rest_7_), channel_id=1, source_target_pairs={{0,6},{2,0},{4,2},{6,4},{1,7},{3,1},{5,3},{7,5},{8,14},{10,8},{12,... | collective-permute-start | bytes 3686408 | tf_op jit(solution)/shard_map/ppermute | solution.py:347
  164.5 7.6 %collective-permute-start.35 = (bf16[4,200,768]{2,1,0:T(8,128)(2,1)}, bf16[4,200,768]{2,1,0:T(8,128)(2,1)S(1)}, u32[]{:S(2)}, u32[]{:S(2)}) collective-permute-start(bf16[4,200,768]{2,1,0:T(8,128)(2,1)} %collective-permute-done.31.rest_3_), channel_id=1, source_target_pairs={{0,1},{1,0},{2,3},{3,2},{4,5},{5,4},{6,7},{7,6},{8,9},{9,8},{10,11... | collective-permute-start | bytes 3686408 | tf_op jit(solution)/shard_map/ppermute | solution.py:347
  186.6 6.5 %collective-permute-start.36 = (f32[1152,768]{1,0:T(8,128)}, f32[1152,768]{1,0:T(8,128)S(1)}, u32[]{:S(2)}, u32[]{:S(2)}) collective-permute-start(f32[1152,768]{1,0:T(8,128)} %get-tuple-element.62), channel_id=1, source_target_pairs={{0,1},{1,0},{2,3},{3,2},{4,5},{5,4},{6,7},{7,6},{8,9},{9,8},{10,11... | collective-permute-start | bytes 10616840 | tf_op jit(solution)/shard_map/ppermute | solution.py:406
  195.6 15.3 %collective-permute-start.49 = (f32[96,768]{1,0:T(8,128)S(1)}, f32[96,768]{1,0:T(8,128)S(1)}, u32[]{:S(2)}, u32[]{:S(2)}) collective-permute-start(f32[96,768]{1,0:T(8,128)S(1)} %get-tuple-element.68), channel_id=1, source_target_pairs={{0,2},{2,4},{4,6},{6,0},{1,3},{3,5},{5,7},{7,1},{8,10},{10,12},{12... | collective-permute-start | bytes 884744 | tf_op jit(solution)/shard_map/ppermute | solution.py:401
  195.7 21.4 %collective-permute-start.50 = (f32[96,768]{1,0:T(8,128)S(1)}, f32[96,768]{1,0:T(8,128)S(1)}, u32[]{:S(2)}, u32[]{:S(2)}) collective-permute-start(f32[96,768]{1,0:T(8,128)S(1)} %get-tuple-element.70), channel_id=1, source_target_pairs={{0,4},{2,6},{4,0},{6,2},{1,5},{3,7},{5,1},{7,3},{8,12},{10,14},{12... | collective-permute-start | bytes 884744 | tf_op jit(solution)/shard_map/ppermute | solution.py:401
  203.5 17.7 %collective-permute-start.51 = (f32[96,768]{1,0:T(8,128)S(1)}, f32[96,768]{1,0:T(8,128)S(1)}, u32[]{:S(2)}, u32[]{:S(2)}) collective-permute-start(f32[96,768]{1,0:T(8,128)S(1)} %get-tuple-element.69), channel_id=1, source_target_pairs={{0,6},{2,0},{4,2},{6,4},{1,7},{3,1},{5,3},{7,5},{8,14},{10,8},{12,... | collective-permute-start | bytes 884744 | tf_op jit(solution)/shard_map/ppermute | solution.py:401
  206.8 18.0 %collective-permute-start.40 = (f32[96,768]{1,0:T(8,128)S(1)}, f32[96,768]{1,0:T(8,128)S(1)}, u32[]{:S(2)}, u32[]{:S(2)}) collective-permute-start(f32[96,768]{1,0:T(8,128)S(1)} %get-tuple-element.71), channel_id=1, source_target_pairs={{0,8},{8,16},{16,24},{24,0},{1,9},{9,17},{17,25},{25,1},{2,10},{10... | collective-permute-start | bytes 884744 | tf_op jit(solution)/shard_map/ppermute | solution.py:401
  206.8 18.5 %collective-permute-start.41 = (f32[96,768]{1,0:T(8,128)S(1)}, f32[96,768]{1,0:T(8,128)S(1)}, u32[]{:S(2)}, u32[]{:S(2)}) collective-permute-start(f32[96,768]{1,0:T(8,128)S(1)} %get-tuple-element.73), channel_id=1, source_target_pairs={{0,16},{8,24},{16,0},{24,8},{1,17},{9,25},{17,1},{25,9},{2,18},{10... | collective-permute-start | bytes 884744 | tf_op jit(solution)/shard_map/ppermute | solution.py:401
  210.9 14.5 %collective-permute-start.42 = (f32[96,768]{1,0:T(8,128)S(1)}, f32[96,768]{1,0:T(8,128)S(1)}, u32[]{:S(2)}, u32[]{:S(2)}) collective-permute-start(f32[96,768]{1,0:T(8,128)S(1)} %get-tuple-element.72), channel_id=1, source_target_pairs={{0,24},{8,0},{16,8},{24,16},{1,25},{9,1},{17,9},{25,17},{2,26},{10... | collective-permute-start | bytes 884744 | tf_op jit(solution)/shard_map/ppermute | solution.py:401
  217.0 16.7 %collective-permute-start.37 = (f32[96,768]{1,0:T(8,128)S(1)}, f32[96,768]{1,0:T(8,128)S(1)}, u32[]{:S(2)}, u32[]{:S(2)}) collective-permute-start(f32[96,768]{1,0:T(8,128)S(1)} %get-tuple-element.74), channel_id=1, source_target_pairs={{0,32},{32,64},{64,96},{96,0},{1,33},{33,65},{65,97},{97,1},{2,34}... | collective-permute-start | bytes 884744 | tf_op jit(solution)/shard_map/ppermute | solution.py:401
  221.2 15.9 %collective-permute-start.38 = (f32[96,768]{1,0:T(8,128)S(1)}, f32[96,768]{1,0:T(8,128)S(1)}, u32[]{:S(2)}, u32[]{:S(2)}) collective-permute-start(f32[96,768]{1,0:T(8,128)S(1)} %get-tuple-element.76), channel_id=1, source_target_pairs={{0,64},{32,96},{64,0},{96,32},{1,65},{33,97},{65,1},{97,33},{2,66}... | collective-permute-start | bytes 884744 | tf_op jit(solution)/shard_map/ppermute | solution.py:401
  224.8 12.4 %collective-permute-start.39 = (f32[96,768]{1,0:T(8,128)S(1)}, f32[96,768]{1,0:T(8,128)S(1)}, u32[]{:S(2)}, u32[]{:S(2)}) collective-permute-start(f32[96,768]{1,0:T(8,128)S(1)} %get-tuple-element.75), channel_id=1, source_target_pairs={{0,96},{32,0},{64,32},{96,64},{1,97},{33,1},{65,33},{97,65},{2,98}... | collective-permute-start | bytes 884744 | tf_op jit(solution)/shard_map/ppermute | solution.py:401
  225.4 13.4 %collective-permute-start.52 = (f32[24,768]{1,0:T(8,128)S(1)}, f32[24,768]{1,0:T(8,128)S(1)}, u32[]{:S(2)}, u32[]{:S(2)}) collective-permute-start(f32[24,768]{1,0:T(8,128)S(1)} %get-tuple-element.80), channel_id=1, source_target_pairs={{0,8},{8,16},{16,24},{24,0},{1,9},{9,17},{17,25},{25,1},{2,10},{10... | collective-permute-start | bytes 221192 | tf_op jit(solution)/shard_map/ppermute | solution.py:401
  225.4 15.8 %collective-permute-start.53 = (f32[24,768]{1,0:T(8,128)S(1)}, f32[24,768]{1,0:T(8,128)S(1)}, u32[]{:S(2)}, u32[]{:S(2)}) collective-permute-start(f32[24,768]{1,0:T(8,128)S(1)} %get-tuple-element.82), channel_id=1, source_target_pairs={{0,16},{8,24},{16,0},{24,8},{1,17},{9,25},{17,1},{25,9},{2,18},{10... | collective-permute-start | bytes 221192 | tf_op jit(solution)/shard_map/ppermute | solution.py:401
  233.7 7.6 %collective-permute-start.54 = (f32[24,768]{1,0:T(8,128)S(1)}, f32[24,768]{1,0:T(8,128)S(1)}, u32[]{:S(2)}, u32[]{:S(2)}) collective-permute-start(f32[24,768]{1,0:T(8,128)S(1)} %get-tuple-element.81), channel_id=1, source_target_pairs={{0,24},{8,0},{16,8},{24,16},{1,25},{9,1},{17,9},{25,17},{2,26},{10... | collective-permute-start | bytes 221192 | tf_op jit(solution)/shard_map/ppermute | solution.py:401
  237.3 8.7 %collective-permute-start.43 = (f32[48,768]{1,0:T(8,128)S(1)}, f32[48,768]{1,0:T(8,128)S(1)}, u32[]{:S(2)}, u32[]{:S(2)}) collective-permute-start(f32[48,768]{1,0:T(8,128)S(1)} %get-tuple-element.77), channel_id=1, source_target_pairs={{0,2},{2,4},{4,6},{6,0},{1,3},{3,5},{5,7},{7,1},{8,10},{10,12},{12... | collective-permute-start | bytes 442376 | tf_op jit(solution)/shard_map/ppermute | solution.py:401
  237.3 8.6 %collective-permute-start.44 = (f32[48,768]{1,0:T(8,128)S(1)}, f32[48,768]{1,0:T(8,128)S(1)}, u32[]{:S(2)}, u32[]{:S(2)}) collective-permute-start(f32[48,768]{1,0:T(8,128)S(1)} %get-tuple-element.78), channel_id=1, source_target_pairs={{0,4},{2,6},{4,0},{6,2},{1,5},{3,7},{5,1},{7,3},{8,12},{10,14},{12... | collective-permute-start | bytes 442376 | tf_op jit(solution)/shard_map/ppermute | solution.py:401
  238.7 7.9 %collective-permute-start.45 = (f32[48,768]{1,0:T(8,128)S(1)}, f32[48,768]{1,0:T(8,128)S(1)}, u32[]{:S(2)}, u32[]{:S(2)}) collective-permute-start(f32[48,768]{1,0:T(8,128)S(1)} %get-tuple-element.79), channel_id=1, source_target_pairs={{0,6},{2,0},{4,2},{6,4},{1,7},{3,1},{5,3},{7,5},{8,14},{10,8},{12,... | collective-permute-start | bytes 442376 | tf_op jit(solution)/shard_map/ppermute | solution.py:401
  246.7 12.8 %collective-permute-start.46 = (f32[6,768]{1,0:T(8,128)S(1)}, f32[6,768]{1,0:T(8,128)S(1)}, u32[]{:S(2)}, u32[]{:S(2)}) collective-permute-start(f32[6,768]{1,0:T(8,128)S(1)} %get-tuple-element.88), channel_id=1, source_target_pairs={{0,8},{8,16},{16,24},{24,0},{1,9},{9,17},{17,25},{25,1},{2,10},{10... | collective-permute-start | bytes 55304 | tf_op jit(solution)/shard_map/ppermute | solution.py:401
  246.8 13.7 %collective-permute-start.47 = (f32[6,768]{1,0:T(8,128)S(1)}, f32[6,768]{1,0:T(8,128)S(1)}, u32[]{:S(2)}, u32[]{:S(2)}) collective-permute-start(f32[6,768]{1,0:T(8,128)S(1)} %get-tuple-element.90), channel_id=1, source_target_pairs={{0,16},{8,24},{16,0},{24,8},{1,17},{9,25},{17,1},{25,9},{2,18},{10... | collective-permute-start | bytes 55304 | tf_op jit(solution)/shard_map/ppermute | solution.py:401
  253.5 7.0 %collective-permute-start.48 = (f32[6,768]{1,0:T(8,128)S(1)}, f32[6,768]{1,0:T(8,128)S(1)}, u32[]{:S(2)}, u32[]{:S(2)}) collective-permute-start(f32[6,768]{1,0:T(8,128)S(1)} %get-tuple-element.89), channel_id=1, source_target_pairs={{0,24},{8,0},{16,8},{24,16},{1,25},{9,1},{17,9},{25,17},{2,26},{10... | collective-permute-start | bytes 55304 | tf_op jit(solution)/shard_map/ppermute | solution.py:401
  254.7 6.4 %collective-permute-start.55 = (f32[12,768]{1,0:T(8,128)S(1)}, f32[12,768]{1,0:T(8,128)S(1)}, u32[]{:S(2)}, u32[]{:S(2)}) collective-permute-start(f32[12,768]{1,0:T(8,128)S(1)} %get-tuple-element.83), channel_id=1, source_target_pairs={{0,32},{32,64},{64,96},{96,0},{1,33},{33,65},{65,97},{97,1},{2,34}... | collective-permute-start | bytes 110600 | tf_op jit(solution)/shard_map/ppermute | solution.py:401
  256.1 6.0 %collective-permute-start.56 = (f32[12,768]{1,0:T(8,128)S(1)}, f32[12,768]{1,0:T(8,128)S(1)}, u32[]{:S(2)}, u32[]{:S(2)}) collective-permute-start(f32[12,768]{1,0:T(8,128)S(1)} %get-tuple-element.84), channel_id=1, source_target_pairs={{0,64},{32,96},{64,0},{96,32},{1,65},{33,97},{65,1},{97,33},{2,66}... | collective-permute-start | bytes 110600 | tf_op jit(solution)/shard_map/ppermute | solution.py:401
  (32 other events, 329.7 us)
where the time goes:
time: 265 us; the launch traced here: 264 us
  waiting for transfers between devices  90.5 us (34%)
  starting transfers between devices  88.1 us (33%)
  Pallas kernels  63 us (24%)
  local copies, waits for them, and re-layouts  15 us (6%)
  other arithmetic  6.5 us (2%)
    ppermute x36, waiting for transfers between devices, shift(): return lax.ppermute(x, axis, [(k, (k + step) % n) for k in range(n)])  72.2 us
    ppermute x21, starting transfers between devices, ring_scatter(): lax.ppermute(piece, axis, [(k, (k + step) % n) for k in range(n)])  52.9 us
    pallas_call x3, Pallas kernels, negative_pairs(): pl.pallas_call(functools.partial(negatives_kernel, pairs=pairs, rings=rin...  46.4 us
    ppermute x36, starting transfers between devices, shift(): return lax.ppermute(x, axis, [(k, (k + step) % n) for k in range(n)])  35.2 us
    pallas_call x1, Pallas kernels, own_pairs(): pl.pallas_call(functools.partial(own_kernel, pairs=pairs), name='own_pair...  16.6 us
    ppermute x21, waiting for transfers between devices, ring_scatter(): lax.ppermute(piece, axis, [(k, (k + step) % n) for k in range(n)])  13.2 us
    unnamed x51, local copies, waits for them, and re-layouts  7.88 us
  transfers between devices with their start and end apart: 58, of which 26 were waited for; matrix products, arithmetic and copies ran while one was open for 5% of the time, Pallas kernels for 19%

commit v1 on v0

--- a/solution.py
+++ b/solution.py
@@ -94,7 +94,7 @@
 
 
 def own_kernel(
-    tan_ref, text_ref, qw_ref, image_ref, kvw_ref, head_ref,
+    tan_ref, text_ref, far_text_ref, qw_ref, image_ref, kvw_ref, head_ref,
     qx_ref, mhx_ref, ones_ref, grad_ref, dq_ref, lrow_ref,
     kv_ref, dkv_ref, xt_ref,
     *, pairs,
@@ -102,13 +102,16 @@
     fill_constants(head_ref, mhx_ref, ones_ref)
     dq_ref[...] = jnp.zeros_like(dq_ref)
     dkv_ref[...] = jnp.zeros_like(dkv_ref)
-    queries = (nn(text_ref[...], qw_ref[...]).astype(BF16).astype(F32) * 0.125)
     _, same = block_mask()
-    for t in range(pairs):
-        for g in range(GROUPS):
-            part = queries[t * QP : (t + 1) * QP, g * GW : (g + 1) * GW]
-            wide = jnp.concatenate([part] * 4, axis=0)
-            qx_ref[t * GROUPS + g] = jnp.where(same, wide, 0.0).astype(BF16)
+    real = lax.broadcasted_iota(jnp.int32, (pairs * QP, D), 0) % QP < LT
+    for side, tokens in enumerate((text_ref, far_text_ref)):
+        queries = nn(tokens[...], qw_ref[...]).astype(BF16).astype(F32) * 0.125
+        queries = jnp.where(real, queries, 0.0)
+        for t in range(pairs):
+            for g in range(GROUPS):
+                part = queries[t * QP : (t + 1) * QP, g * GW : (g + 1) * GW]
+                wide = jnp.concatenate([part] * 4, axis=0)
+                qx_ref[(side * pairs + t) * GROUPS + g] = jnp.where(same, wide, 0.0).astype(BF16)
 
     def one(i, carry):
         image = image_ref[i]
@@ -161,27 +164,26 @@
     half = jnp.where((near == 0) | (near == 3), 0, 1)
     row = inner % 2 + jnp.where((near == 2) | (near == 3), 2, 0)
     kind = jnp.where(far == 0, 0, jnp.where(far == 3, 1, jnp.where(far == 1, 2, 3)))
-    other = (owner + spot[2]) % 2
     number = kind * 2 + half
     phase = jnp.where(kind == 3, 2, jnp.where((number == 3) | (number == 4), 1, 0))
-    return (other * 2 + color) * 8 + number, row, phase
+    phase = jnp.where(owner % 2 == spot[2], phase, 3)
+    return color * 8 + number, row, phase
 
 
 def negatives_kernel(
-    pick_ref, tan_ref, spot_ref, text_ref, qx_ref, mhx_ref, ones_ref, kvw_ref, head_ref, dq_in_ref, lrow_in_ref,
+    pick_ref, tan_ref, spot_ref, qx_ref, mhx_ref, ones_ref, kvw_ref, head_ref, dq_in_ref, lrow_in_ref,
     grad_in_ref, *rest,
     pairs, rings, blocks, phase,
 ):
     last = phase == 2
     pieces, rest = rest[: len(blocks)], rest[len(blocks) :]
     if last:
-        mine_ref, other_ref, lrow_ref = rest[:3]
+        mine_ref, other_ref, own_dq_ref, give_ref, lrow_ref = rest[:5]
+        rest = rest[5:]
     else:
-        out_grad_ref, out_dq_ref, lrow_ref = rest[:3]
-    (
-        kv_ref, dkv_ref, xt_ref, image_ref, grad_ref, prior_ref, dq_ref, out_ref, list_ref,
-        sems, prior_sem, out_sems,
-    ) = rest[3:]
+        out_grad_ref, dq_ref, lrow_ref = rest[:3]
+        rest = rest[3:] + (dq_ref,)
+    kv_ref, dkv_ref, xt_ref, image_ref, prior_ref, out_ref, list_ref, sems, prior_sem, out_sems, dq_ref = rest
     spot = [spot_ref[k] for k in range(3)]
     count = jnp.int32(0)
     for j in range(pairs):
@@ -239,42 +241,57 @@
 
         lax.fori_loop(0, twos, two, 0)
 
+    prior.wait()
     if not last:
-        prior.wait()
-        products(0)
-        products(1)
-        out_grad_ref[...] = prior_ref[...]
-        out_dq_ref[...] = dq_ref[...]
-        return
-
-    core = spot[2]
+        copies = []
+        for part in range(2):
+            products(part)
+            cols = pl.ds(part * D, D)
+            copies.append(
+                pltpu.make_async_copy(prior_ref.at[:, cols], out_grad_ref.at[:, cols], out_sems.at[part])
+            )
+            copies[-1].start()
+    else:
+        rows = own_dq_ref.shape[0]
+        own_dq_ref[...] = dq_ref[:rows]
+        give_ref[:rows] = dq_ref[rows:]
+        give_ref[rows:] = jnp.zeros((pairs // 2, D), F32)
+        give_ref[rows:, :GW] = lrow_ref[pairs // 2 :]
+        copies = []
+        for part in range(2):
+            products(part)
+            copies += spread(part + 1, part, prior_ref, part * D, out_ref, mine_ref, other_ref, out_sems, spot[2], rings)
+    for copy in copies:
+        copy.wait()
+
+
+def spread(color, place, source_ref, lo, out_ref, mine_ref, other_ref, sems, core, rings):
     half = D // 2
-
-    def spread(color, source_ref, lo):
-        size, strips = strip_rows(color, rings)
-        for which, source, target in strips:
-            slot = jnp.where(core == which, 0, 1)
-            out_ref[slot, color * half + target : color * half + target + size, :] = source_ref[
-                source : source + size, lo : lo + D
-            ]
-        copies = []
-        for slot, ref in ((1, other_ref), (0, mine_ref)):
-            copy = pltpu.make_async_copy(
-                out_ref.at[slot, pl.ds(color * half, half)],
-                ref.at[pl.ds(color * half, half)],
-                out_sems.at[2 * color + slot],
-            )
-            copy.start()
-            copies.append(copy)
-        return copies
-
-    grad_ref[...] = tn(text_ref[...], dq_ref[...].astype(BF16))
-    copies = spread(0, grad_ref, 0)
-    prior.wait()
-    for part in range(2):
-        products(part)
-        copies += spread(part + 1, prior_ref, part * D)
-    for copy in copies:
+    size, strips = strip_rows(color, rings)
+    for which, source, target in strips:
+        slot = jnp.where(core == which, 0, 1)
+        out_ref[slot, place * half + target : place * half + target + size, :] = source_ref[
+            source : source + size, lo : lo + D
+        ]
+    copies = []
+    for slot, ref in ((1, other_ref), (0, mine_ref)):
+        copy = pltpu.make_async_copy(
+            out_ref.at[slot, pl.ds(place * half, half)],
+            ref.at[pl.ds(place * half, half)],
+            sems.at[2 * place + slot],
+        )
+        copy.start()
+        copies.append(copy)
+    return copies
+
+
+def query_kernel(
+    spot_ref, text_ref, dq_ref, got_ref, mine_ref, other_ref, grad_ref, out_ref, sems, *, rings
+):
+    rows = text_ref.shape[0]
+    total = dq_ref[:rows] + got_ref[:rows]
+    grad_ref[...] = tn(text_ref[...], total.astype(BF16))
+    for copy in spread(0, 0, grad_ref, 0, out_ref, mine_ref, other_ref, sems, spot_ref[2], rings):
         copy.wait()
 
 
@@ -284,19 +301,19 @@
 LIMIT = 60 * 1024 * 1024
 
 
-def own_pairs(tangent, text, query_weight, images, kv_weight, head):
+def own_pairs(tangent, text, far_text, query_weight, images, kv_weight, head):
     pairs = images.shape[0]
     return pl.pallas_call(
         functools.partial(own_kernel, pairs=pairs),
         name="own_pairs",
-        in_specs=[SM] + [VM] * 5,
+        in_specs=[SM] + [VM] * 6,
         out_specs=[VM] * 6,
         out_shape=[
-            jax.ShapeDtypeStruct((pairs * GROUPS, ROWS, GW), BF16),
+            jax.ShapeDtypeStruct((2 * pairs * GROUPS, ROWS, GW), BF16),
             jax.ShapeDtypeStruct((3 * GROUPS, ROWS, GW), BF16),
             jax.ShapeDtypeStruct((ROWS, GW), BF16),
             jax.ShapeDtypeStruct((D, 2 * D), F32),
-            jax.ShapeDtypeStruct((pairs * QP, D), F32),
+            jax.ShapeDtypeStruct((2 * pairs * QP, D), F32),
             jax.ShapeDtypeStruct((pairs, GW), F32),
         ],
         scratch_shapes=[
@@ -305,41 +322,65 @@
             pltpu.VMEM((D, pairs * LX), BF16),
         ],
         compiler_params=pltpu.CompilerParams(vmem_limit_bytes=LIMIT),
-    )(tangent, text, query_weight, images, kv_weight, head)
-
-
-def negative_pairs(picks, tangent, spot, text, made, kv_weight, head, dq, lrow, grad, arrived, rings, phase):
+    )(tangent, text, far_text, query_weight, images, kv_weight, head)
+
+
+def negative_pairs(picks, tangent, spot, made, kv_weight, head, dq, lrow, grad, arrived, rings, phase):
     last = phase == 2
     pairs = picks.shape[0]
     blocks = tuple(arrived)
-    half = jax.ShapeDtypeStruct((3 * D // 2, D), F32)
-    rows = jax.ShapeDtypeStruct(lrow.shape, F32)
+    lrow_shape = jax.ShapeDtypeStruct(lrow.shape, F32)
+    own_rows = dq.shape[0] // 2
     if last:
-        out_shape, out_specs = [half, half, rows], [ANY, ANY, VM]
+        in_hbm = 2
+        out_shape = [
+            jax.ShapeDtypeStruct((D, D), F32),
+            jax.ShapeDtypeStruct((D, D), F32),
+            jax.ShapeDtypeStruct((own_rows, D), F32),
+            jax.ShapeDtypeStruct((own_rows + pairs // 2, D), F32),
+            lrow_shape,
+        ]
     else:
-        out_shape = [jax.ShapeDtypeStruct(grad.shape, F32), jax.ShapeDtypeStruct(dq.shape, F32), rows]
-        out_specs = [VM] * 3
+        in_hbm = 1
+        out_shape = [
+            jax.ShapeDtypeStruct(grad.shape, F32), jax.ShapeDtypeStruct(dq.shape, F32), lrow_shape
+        ]
     return pl.pallas_call(
         functools.partial(negatives_kernel, pairs=pairs, rings=rings, blocks=blocks, phase=phase),
-        in_specs=[SM] * 3 + [VM] * 8 + [ANY] * (1 + len(blocks)),
-        out_specs=out_specs,
+        in_specs=[SM] * 3 + [VM] * 7 + [ANY] * (1 + len(blocks)),
+        out_specs=[ANY] * in_hbm + [VM] * (len(out_shape) - in_hbm),
         out_shape=out_shape,
         scratch_shapes=[
             pltpu.VMEM((LP, 2 * D), BF16),
             pltpu.VMEM((pairs * LX, 2 * D), BF16),
             pltpu.VMEM((pairs, D, LX), BF16),
             pltpu.VMEM((pairs, LP, D), BF16),
-            pltpu.VMEM((D, D) if last else (8, 128), F32),
             pltpu.VMEM((D, 2 * D), F32),
-            pltpu.VMEM(dq.shape, F32),
-            pltpu.VMEM((2, 3 * D // 2, D) if last else (2, 8, 128), F32),
+            pltpu.VMEM((2, D, D) if last else (2, 8, 128), F32),
             pltpu.SMEM((pairs + 1,), jnp.int32),
             pltpu.SemaphoreType.DMA((pairs + 1,)),
             pltpu.SemaphoreType.DMA(()),
-            pltpu.SemaphoreType.DMA((6,)),
+            pltpu.SemaphoreType.DMA((4,)),
+        ]
+        + ([pltpu.VMEM(dq.shape, F32)] if last else []),
+        compiler_params=pltpu.CompilerParams(vmem_limit_bytes=LIMIT),
+    )(picks, tangent, spot, *made, kv_weight, head, dq, lrow, grad, *arrived.values())
+
+
+def query_gradient(spot, text, dq, got, rings):
+    return pl.pallas_call(
+        functools.partial(query_kernel, rings=rings),
+        name="query_gradient",
+        in_specs=[SM] + [VM] * 3,
+        out_specs=[ANY] * 2,
+        out_shape=[jax.ShapeDtypeStruct((D // 2, D), F32)] * 2,
+        scratch_shapes=[
+            pltpu.VMEM((D, D), F32),
+            pltpu.VMEM((2, D // 2, D), F32),
+            pltpu.SemaphoreType.DMA((2,)),
         ],
         compiler_params=pltpu.CompilerParams(vmem_limit_bytes=LIMIT),
-    )(picks, tangent, spot, text, *made, kv_weight, head, dq, lrow, grad, *arrived.values())
+    )(spot, text, dq, got)
 
 
 def shift(x, axis, step):
@@ -358,8 +399,8 @@
     return blocks
 
 
-def other_core(blocks):
-    return blocks | {16 + k: shift(block, "dev_2", 1) for k, block in blocks.items()}
+def swapped(x):
+    return lax.ppermute(x, "dev_2", [(0, 1), (1, 0)])
 
 
 def next_steps(first):
@@ -402,13 +443,8 @@
     return sent, lax.dynamic_index_in_dim(blocks, me, 0, keepdims=False)
 
 
-def reduce_gradients(mine, other):
-    from_core = lax.ppermute(other, "dev_2", [(0, 1), (1, 0)])
-    half = mine.shape[0] // 3
-    parts = [
-        mine[k * half : (k + 1) * half] + from_core[k * half : (k + 1) * half] for k in range(3)
-    ]
-    width = mine.shape[1]
+def reduce_gradients(parts, held):
+    width = parts[0].shape[1]
     for stage in range(3):
         moved = []
         for ring, axis in enumerate(RINGS):
@@ -424,41 +460,60 @@
                 kept = kept + piece
             for place, k in enumerate(colors):
                 parts[k] = kept[place * rows : (place + 1) * rows]
-    return parts
+        if stage == 0:
+            parts[2], *held = lax.optimization_barrier((parts[2], *held))
+    return parts, held
 
 
 def local(image_tokens, text_tokens, negatives, query_weight, kv_weight, match_head, cotangent):
     pairs, text_len, model = text_tokens.shape
     images = jnp.pad(image_tokens, ((0, 0), (0, LP - LI), (0, 0)))
+    notes = jnp.concatenate([cotangent, negatives.astype(BF16)], axis=1)
+    notes = jnp.pad(notes[:, None, :], ((0, 0), (0, QP - LT - 1), (0, model - notes.shape[1])))
+    far_text = swapped(jnp.concatenate([text_tokens, notes], axis=1))
+    far_notes = far_text[:, LT, : cotangent.shape[1] + negatives.shape[1]]
     first = first_steps(images)
     text = jnp.pad(text_tokens, ((0, 0), (0, QP - LT), (0, 0))).reshape(pairs * QP, model)
-    scale = cotangent.astype(F32) / text_len
+    both = jnp.concatenate([cotangent, far_notes[:, : cotangent.shape[1]]], axis=0)
+    scale = both.astype(F32) / text_len
     head = match_head.reshape(1, model)
-    *made, grad, dq, own_rows = own_pairs(scale[:, 0], text, query_weight, images, kv_weight, head)
+    *made, grad, dq, own_rows = own_pairs(
+        scale[:pairs, 0], text, far_text.reshape(pairs * QP, model), query_weight, images, kv_weight, head
+    )
     soon, then = next_steps(first)
     passed, dq = together({k: v for k, v in soon.items() if k % 8 in (2, 5)}, dq)
     soon |= passed
     far_blocks = last_steps(soon)
     spot = jnp.stack([lax.axis_index(axis) for axis in DEV]).astype(jnp.int32)
     rings = tuple(lax.axis_size(ring) for ring in RINGS)
-    picks = negatives.reshape(-1)
+    far_negatives = far_notes[:, cotangent.shape[1] :].astype(jnp.int32)
+    picks = jnp.concatenate([negatives, far_negatives], axis=0).reshape(-1)
     far_scale = scale[:, 1:].reshape(-1)
     rows = jnp.zeros((picks.shape[0], GW), F32)
     grad, dq, rows = negative_pairs(
-        picks, far_scale, spot, text, made, kv_weight, head, dq, rows, grad, other_core(soon), rings, 0
+        picks, far_scale, spot, made, kv_weight, head, dq, rows, grad, soon, rings, 0
     )
     then, dq = together(then, dq)
     grad, dq, rows = negative_pairs(
-        picks, far_scale, spot, text, made, kv_weight, head, dq, rows, grad, other_core(then), rings, 1
-    )
-    far_blocks, dq = together(far_blocks, dq)
-    mine, other, rows = negative_pairs(
-        picks, far_scale, spot, text, made, kv_weight, head, dq, rows, grad, other_core(far_blocks), rings, 2
-    )
+        picks, far_scale, spot, made, kv_weight, head, dq, rows, grad, then, rings, 1
+    )
+    mine, other, dq, give, rows = negative_pairs(
+        picks, far_scale, spot, made, kv_weight, head, dq, rows, grad, far_blocks, rings, 2
+    )
+    got = swapped(give)
+    from_core = swapped(other)
+    rest = mine.shape[0] // 2
+    key_part, value_part, got = lax.optimization_barrier(
+        (mine[:rest] + from_core[:rest], mine[rest:] + from_core[rest:], got)
+    )
+    mine_query, other_query = query_gradient(spot, text, dq, got, rings)
+    parts = [mine_query + swapped(other_query), key_part, value_part]
+    (grad_query, grad_key, grad_value), (rows, got) = reduce_gradients(parts, (rows, got))
+    half = picks.shape[0] // 2
+    rows = rows[:half] + got[pairs * QP :, :GW]
     own_logits = jnp.sum(own_rows, axis=1, keepdims=True)
     far_logits = jnp.sum(rows, axis=1).reshape(pairs, 2)
     logits = jnp.concatenate([own_logits, far_logits], axis=1) / text_len
-    grad_query, grad_key, grad_value = reduce_gradients(mine, other)
     return logits, grad_query, jnp.concatenate([grad_key, grad_value], axis=1)
 
 

time: 265 us -> 267 us (level)
  the two profiles are of different devices: /device:TPU:0 before, /device:TPU:110 now
where the time goes in v1:
time: 267 us; the launch traced here: 262 us
  waiting for transfers between devices  89.6 us (34%)
  Pallas kernels  69.6 us (26%)
  starting transfers between devices  65.5 us (25%)
  local copies, waits for them, and re-layouts  23.1 us (9%)
  other arithmetic  13.2 us (5%)
    ppermute x20, waiting for transfers between devices, shift(): return lax.ppermute(x, axis, [(k, (k + step) % n) for k in range(n)])  58.6 us
    pallas_call x3, Pallas kernels, negative_pairs(): pl.pallas_call(functools.partial(negatives_kernel, pairs=pairs, rings=rin...  48.9 us
    ppermute x21, starting transfers between devices, ring_scatter(): lax.ppermute(piece, axis, [(k, (k + step) % n) for k in range(n)])  41.1 us
    ppermute x21, waiting for transfers between devices, ring_scatter(): lax.ppermute(piece, axis, [(k, (k + step) % n) for k in range(n)])  26.8 us
    ppermute x20, starting transfers between devices, shift(): return lax.ppermute(x, axis, [(k, (k + step) % n) for k in range(n)])  23.6 us
    pallas_call x1, Pallas kernels, own_pairs(): pl.pallas_call(functools.partial(own_kernel, pairs=pairs), name='own_pair...  17.2 us
    unnamed x37, local copies, waits for them, and re-layouts  9.81 us
  transfers between devices with their start and end apart: 45, of which 20 were waited for; matrix products, arithmetic and copies ran while one was open for 12% of the time, Pallas kernels for 18%

profile of v1, /device:TPU:110, one launch (start us, length us, event | category | flops | bytes accessed | tf_op | source)
XLA Modules:
  0.0 261.9 jit_solution(14436501063790174632)
XLA Ops:
  0.6 1.4 copy.32
  3.0 1.6 collective-permute-start.1
  4.5 2.0 collective-permute-start.9
  6.6 12.0 %collective-permute-done.1 = bf16[2,200,768]{2,1,0:T(8,128)(2,1)S(1)} collective-permute-done((bf16[2,200,768]{2,1,0:T(8,128)(2,1)S(1)}, bf16[2,200,768]{2,1,0:T(8,128)(2,1)S(1)}, u32[]{:S(2)}, u32[]{:S(2)}) %collective-permute-start.1) | collective-permute-done | bytes 614432 | tf_op jit(solution)/shard_map/ppermute | solution.py:388
  20.1 2.5 pad_maximum_fusion.1.rest_4_
  22.5 1.3 collective-permute-start.8
  25.7 1.6 collective-permute-start.10
  29.0 1.9 constant_dynamic-update-slice_fusion.5
  31.0 7.3 %collective-permute-done.3 = bf16[2,200,768]{2,1,0:T(8,128)(2,1)} collective-permute-done((bf16[2,200,768]{2,1,0:T(8,128)(2,1)S(1)}, bf16[2,200,768]{2,1,0:T(8,128)(2,1)}, u32[]{:S(2)}, u32[]{:S(2)}) %collective-permute-start.3) | collective-permute-done | bytes 614432 | tf_op jit(solution)/shard_map/ppermute | solution.py:388
  40.3 1.9 constant_dynamic-update-slice_fusion.2
  42.3 11.1 %collective-permute-done.10 = bf16[1,200,768]{2,1,0:T(8,128)(2,1)S(1)} collective-permute-done((bf16[1,200,768]{2,1,0:T(8,128)(2,1)S(1)}, bf16[1,200,768]{2,1,0:T(8,128)(2,1)S(1)}, u32[]{:S(2)}, u32[]{:S(2)}) %collective-permute-start.10) | collective-permute-done | bytes 307232 | tf_op jit(solution)/shard_map/ppermute | solution.py:388
  53.4 1.8 collective-permute-start.5
  57.1 2.5 collective-permute-start.12
  60.4 1.4 collective-permute-done.5
  63.2 1.9 collective-permute-start.16
  65.1 3.1 %collective-permute-start.13 = (bf16[4,200,768]{2,1,0:T(8,128)(2,1)}, bf16[4,200,768]{2,1,0:T(8,128)(2,1)}, u32[]{:S(2)}, u32[]{:S(2)}) collective-permute-start(bf16[4,200,768]{2,1,0:T(8,128)(2,1)} %constant_dynamic-update-slice_fusion.rest_1_), channel_id=1, source_target_pairs={{0,8},{8,16},{16,24},{24,0},{1,9},{9,17},{17,25},{25,1},{2,10},{10... | collective-permute-start | bytes 3686408 | tf_op jit(solution)/shard_map/ppermute | solution.py:388
  72.0 17.2 %own_pairs.1 = (bf16[24,128,256]{2,1,0:T(8,128)(2,1)}, bf16[9,128,256]{2,1,0:T(8,128)(2,1)}, bf16[128,256]{1,0:T(8,128)(2,1)}, f32[768,1536]{1,0:T(8,128)}, f32[256,768]{1,0:T(8,128)}, /*index=5*/f32[4,256]{1,0:T(4,128)}) custom-call(f32[4]{0:T(128)} %slice_reduce_fusion.tan_ref, bf16[128,768]{1,0:T(8,128)(2,1)} %bitcast.115, bf16[128,768]{1,0:T(8,128)(2,1)} %bitcast.119, ...), custom_call_target="tpu_custom_call" | custom-call | tf_op jit(solution)/shard_map/own_pairs/pallas_call | solution.py:306
  89.2 1.9 collective-permute-start.15
  91.1 2.8 %collective-permute-done.6.rest_3_ = bf16[4,200,768]{2,1,0:T(8,128)(2,1)} collective-permute-done((bf16[4,200,768]{2,1,0:T(8,128)(2,1)}, bf16[4,200,768]{2,1,0:T(8,128)(2,1)}, u32[]{:S(2)}, u32[]{:S(2)}) %collective-permute-start.6) | collective-permute-done | bytes 1228832 | tf_op jit(solution)/shard_map/ppermute | solution.py:388
  94.6 22.3 %collective-permute-done.14.rest_1_ = bf16[4,200,768]{2,1,0:T(8,128)(2,1)} collective-permute-done((bf16[4,200,768]{2,1,0:T(8,128)(2,1)S(1)}, bf16[4,200,768]{2,1,0:T(8,128)(2,1)}, u32[]{:S(2)}, u32[]{:S(2)}) %collective-permute-start.14) | collective-permute-done | bytes 1228832 | tf_op jit(solution)/shard_map/ppermute | solution.py:388
  116.9 2.1 collective-permute-start.19
  121.5 18.6 %shard_map.94 = (f32[768,1536]{1,0:T(8,128)}, f32[256,768]{1,0:T(8,128)}, f32[16,256]{1,0:T(8,128)}) custom-call(s32[16]{0:T(128)} %reshape.54.pick_ref, f32[16]{0:T(128)} %reshape.55.tan_ref, s32[3]{0:T(128)} %pad_add_fusion.1.spot_ref, bf16[24,128,256]{2,1,0:T(8,128)(2,1)} %get-tuple-element.39.qx_ref, bf16[9,128,256]{2,1,0:T(8,128)(2,1)} %get-tuple-element.40.mhx_ref, ...), custom_call_target="tpu_custom_call" | custom-call | tf_op jit(solution)/shard_map/pallas_call | solution.py:348
  140.2 10.7 %shard_map.95 = (f32[768,1536]{1,0:T(8,128)}, f32[256,768]{1,0:T(8,128)}, f32[16,256]{1,0:T(8,128)}) custom-call(s32[16]{0:T(128)} %reshape.54.pick_ref, f32[16]{0:T(128)} %reshape.55.tan_ref, s32[3]{0:T(128)} %pad_add_fusion.1.spot_ref, bf16[24,128,256]{2,1,0:T(8,128)(2,1)} %get-tuple-element.39.qx_ref, bf16[9,128,256]{2,1,0:T(8,128)(2,1)} %get-tuple-element.40.mhx_ref, ...), custom_call_target="tpu_custom_call" | custom-call | tf_op jit(solution)/shard_map/pallas_call | solution.py:348
  152.3 19.6 %shard_map.96 = (f32[768,768]{1,0:T(8,128)}, f32[768,768]{1,0:T(8,128)}, f32[128,768]{1,0:T(8,128)}, f32[136,768]{1,0:T(8,128)}, f32[16,256]{1,0:T(8,128)}) custom-call(s32[16]{0:T(128)} %reshape.54.pick_ref, f32[16]{0:T(128)} %reshape.55.tan_ref, s32[3]{0:T(128)} %pad_add_fusion.1.spot_ref, bf16[24,128,256]{2,1,0:T(8,128)(2,1)} %get-tuple-element.39.qx_ref, ...), custom_call_target="tpu_custom_call" | custom-call | tf_op jit(solution)/shard_map/pallas_call | solution.py:348
  172.6 4.2 %collective-permute-done.21 = f32[768,768]{1,0:T(8,128)S(1)} collective-permute-done((f32[768,768]{1,0:T(8,128)}, f32[768,768]{1,0:T(8,128)S(1)}, u32[]{:S(2)}, u32[]{:S(2)}) %collective-permute-start.21) | collective-permute-done | bytes 2359328 | tf_op jit(solution)/shard_map/ppermute | solution.py:403
  176.8 1.9 slice_add_fusion
  179.5 3.4 %query_gradient.1 = (f32[384,768]{1,0:T(8,128)}, f32[384,768]{1,0:T(8,128)}) custom-call(s32[3]{0:T(128)} %pad_add_fusion.1.spot_ref, bf16[128,768]{1,0:T(8,128)(2,1)} %bitcast.116, f32[128,768]{1,0:T(8,128)} %get-tuple-element.68.dq_ref, f32[136,768]{1,0:T(8,128)} %copy-done.9), custom_call_target="tpu_custom_call" | custom-call | tf_op jit(solution)/shard_map/query_gradient/pallas_call | solution.py:371
  184.1 10.7 %collective-permute-start.24 = (f32[96,768]{1,0:T(8,128)}, f32[96,768]{1,0:T(8,128)}, u32[]{:S(2)}, u32[]{:S(2)}) collective-permute-start(f32[96,768]{1,0:T(8,128)} %get-tuple-element.85), channel_id=1, source_target_pairs={{0,4},{2,6},{4,0},{6,2},{1,5},{3,7},{5,1},{7,3},{8,12},{10,14},{12... | collective-permute-start | bytes 884744 | tf_op jit(solution)/shard_map/ppermute | solution.py:442
  196.0 4.9 %collective-permute-done.23 = f32[96,768]{1,0:T(8,128)} collective-permute-done((f32[96,768]{1,0:T(8,128)}, f32[96,768]{1,0:T(8,128)}, u32[]{:S(2)}, u32[]{:S(2)}) %collective-permute-start.23) | collective-permute-done | bytes 294944 | tf_op jit(solution)/shard_map/ppermute | solution.py:442
  200.9 2.1 collective-permute-done.24
  204.3 4.2 %collective-permute-done.25 = f32[96,768]{1,0:T(8,128)} collective-permute-done((f32[96,768]{1,0:T(8,128)}, f32[96,768]{1,0:T(8,128)}, u32[]{:S(2)}, u32[]{:S(2)}) %collective-permute-start.25) | collective-permute-done | bytes 294944 | tf_op jit(solution)/shard_map/ppermute | solution.py:442
  211.3 1.4 add.233
  212.8 6.7 %collective-permute-start.27 = (f32[96,768]{1,0:T(8,128)S(1)}, f32[96,768]{1,0:T(8,128)S(1)}, u32[]{:S(2)}, u32[]{:S(2)}) collective-permute-start(f32[96,768]{1,0:T(8,128)S(1)} %get-tuple-element.80), channel_id=1, source_target_pairs={{0,32},{32,64},{64,96},{96,0},{1,33},{33,65},{65,97},{97,1},{2,34}... | collective-permute-start | bytes 884744 | tf_op jit(solution)/shard_map/ppermute | solution.py:442
  219.5 5.1 %collective-permute-start.28 = (f32[96,768]{1,0:T(8,128)S(1)}, f32[96,768]{1,0:T(8,128)S(1)}, u32[]{:S(2)}, u32[]{:S(2)}) collective-permute-start(f32[96,768]{1,0:T(8,128)S(1)} %get-tuple-element.82), channel_id=1, source_target_pairs={{0,64},{32,96},{64,0},{96,32},{1,65},{33,97},{65,1},{97,33},{2,66}... | collective-permute-start | bytes 884744 | tf_op jit(solution)/shard_map/ppermute | solution.py:442
  225.3 2.7 %collective-permute-start.39 = (f32[24,768]{1,0:T(8,128)S(1)}, f32[24,768]{1,0:T(8,128)S(1)}, u32[]{:S(2)}, u32[]{:S(2)}) collective-permute-start(f32[24,768]{1,0:T(8,128)S(1)} %get-tuple-element.89), channel_id=1, source_target_pairs={{0,8},{8,16},{16,24},{24,0},{1,9},{9,17},{17,25},{25,1},{2,10},{10... | collective-permute-start | bytes 221192 | tf_op jit(solution)/shard_map/ppermute | solution.py:442
  228.0 1.6 collective-permute-start.40
  230.7 1.8 collective-permute-start.41
  232.6 4.5 %collective-permute-done.29 = f32[96,768]{1,0:T(8,128)S(1)} collective-permute-done((f32[96,768]{1,0:T(8,128)S(1)}, f32[96,768]{1,0:T(8,128)S(1)}, u32[]{:S(2)}, u32[]{:S(2)}) %collective-permute-start.29) | collective-permute-done | bytes 294944 | tf_op jit(solution)/shard_map/ppermute | solution.py:442
  237.2 2.5 collective-permute-start.33
  239.7 2.7 %collective-permute-start.34 = (f32[48,768]{1,0:T(8,128)S(1)}, f32[48,768]{1,0:T(8,128)S(1)}, u32[]{:S(2)}, u32[]{:S(2)}) collective-permute-start(f32[48,768]{1,0:T(8,128)S(1)} %get-tuple-element.87), channel_id=1, source_target_pairs={{0,4},{2,6},{4,0},{6,2},{1,5},{3,7},{5,1},{7,3},{8,12},{10,14},{12... | collective-permute-start | bytes 442376 | tf_op jit(solution)/shard_map/ppermute | solution.py:442
  243.4 1.7 collective-permute-done.33
  245.0 2.9 %collective-permute-done.34 = f32[48,768]{1,0:T(8,128)S(1)} collective-permute-done((f32[48,768]{1,0:T(8,128)S(1)}, f32[48,768]{1,0:T(8,128)S(1)}, u32[]{:S(2)}, u32[]{:S(2)}) %collective-permute-start.34) | collective-permute-done | bytes 147488 | tf_op jit(solution)/shard_map/ppermute | solution.py:442
  248.0 1.8 collective-permute-done.35
  249.9 1.5 collective-permute-start.36
  251.3 2.0 collective-permute-start.37
  253.6 2.4 collective-permute-start.43
  256.7 1.7 collective-permute-done.38
  259.6 1.7 collective-permute-done.44
  (137 shorter events, 34.3 us)
Async XLA Ops:
  3.0 15.6 %collective-permute-start.1 = (bf16[2,200,768]{2,1,0:T(8,128)(2,1)S(1)}, bf16[2,200,768]{2,1,0:T(8,128)(2,1)S(1)}, u32[]{:S(2)}, u32[]{:S(2)}) collective-permute-start(bf16[2,200,768]{2,1,0:T(8,128)(2,1)S(1)} %get-tuple-element.76), channel_id=1, source_target_pairs={{0,2},{2,4},{4,6},{6,0},{1,3},{3,5},{5,7},{7,1},{8,10},{10,12},{12... | collective-permute-start | bytes 1843208 | tf_op jit(solution)/shard_map/ppermute | solution.py:388
  4.5 15.5 %collective-permute-start.7 = (bf16[2,200,768]{2,1,0:T(8,128)(2,1)}, bf16[2,200,768]{2,1,0:T(8,128)(2,1)S(1)}, u32[]{:S(2)}, u32[]{:S(2)}) collective-permute-start(bf16[2,200,768]{2,1,0:T(8,128)(2,1)} %get-tuple-element.75), channel_id=1, source_target_pairs={{0,8},{8,16},{16,24},{24,0},{1,9},{9,17},{17,25},{25,1},{2,10},{10... | collective-permute-start | bytes 1843208 | tf_op jit(solution)/shard_map/ppermute | solution.py:388
  4.5 22.9 %collective-permute-start.9 = (bf16[2,200,768]{2,1,0:T(8,128)(2,1)}, bf16[2,200,768]{2,1,0:T(8,128)(2,1)}, u32[]{:S(2)}, u32[]{:S(2)}) collective-permute-start(bf16[2,200,768]{2,1,0:T(8,128)(2,1)} %get-tuple-element.75), channel_id=1, source_target_pairs={{0,24},{8,0},{16,8},{24,16},{1,25},{9,1},{17,9},{25,17},{2,26},{10... | collective-permute-start | bytes 1843208 | tf_op jit(solution)/shard_map/ppermute | solution.py:388
  18.7 44.4 %copy-start = (bf16[4,200,768]{2,1,0:T(8,128)(2,1)}, bf16[4,200,768]{2,1,0:T(8,128)(2,1)S(1)}, u32[]{:S(2)}) copy-start(bf16[4,200,768]{2,1,0:T(8,128)(2,1)S(1)} %pad_maximum_fusion.rest_0_) | copy-start | bytes 3686404
  18.7 44.5 %collective-permute-start.2 = (bf16[4,200,768]{2,1,0:T(8,128)(2,1)S(1)}, bf16[4,200,768]{2,1,0:T(8,128)(2,1)}, u32[]{:S(2)}, u32[]{:S(2)}) collective-permute-start(bf16[4,200,768]{2,1,0:T(8,128)(2,1)S(1)} %pad_maximum_fusion.rest_0_), channel_id=1, source_target_pairs={{0,8},{8,16},{16,24},{24,0},{1,9},{9,17},{17,25},{25,1},{2,10},{10... | collective-permute-start | bytes 3686408 | tf_op jit(solution)/shard_map/ppermute | solution.py:388
  22.5 42.6 %collective-permute-start.8 = (bf16[4,200,768]{2,1,0:T(8,128)(2,1)}, bf16[4,200,768]{2,1,0:T(8,128)(2,1)}, u32[]{:S(2)}, u32[]{:S(2)}) collective-permute-start(bf16[4,200,768]{2,1,0:T(8,128)(2,1)} %pad_maximum_fusion.1.rest_4_), channel_id=1, source_target_pairs={{0,2},{2,4},{4,6},{6,0},{1,3},{3,5},{5,7},{7,1},{8,10},{10,12},{12... | collective-permute-start | bytes 3686408 | tf_op jit(solution)/shard_map/ppermute | solution.py:388
  23.8 14.4 %collective-permute-start.3 = (bf16[2,200,768]{2,1,0:T(8,128)(2,1)S(1)}, bf16[2,200,768]{2,1,0:T(8,128)(2,1)}, u32[]{:S(2)}, u32[]{:S(2)}) collective-permute-start(bf16[2,200,768]{2,1,0:T(8,128)(2,1)S(1)} %get-tuple-element.76), channel_id=1, source_target_pairs={{0,6},{2,0},{4,2},{6,4},{1,7},{3,1},{5,3},{7,5},{8,14},{10,8},{12,... | collective-permute-start | bytes 1843208 | tf_op jit(solution)/shard_map/ppermute | solution.py:388
  25.7 27.6 %collective-permute-start.10 = (bf16[1,200,768]{2,1,0:T(8,128)(2,1)S(1)}, bf16[1,200,768]{2,1,0:T(8,128)(2,1)S(1)}, u32[]{:S(2)}, u32[]{:S(2)}) collective-permute-start(bf16[1,200,768]{2,1,0:T(8,128)(2,1)S(1)} %slice.87), channel_id=1, source_target_pairs={{0,8},{8,16},{16,24},{24,0},{1,9},{9,17},{17,25},{25,1},{2,10},{10... | collective-permute-start | bytes 921608 | tf_op jit(solution)/shard_map/ppermute | solution.py:388
  28.4 27.5 %collective-permute-start.11 = (bf16[1,200,768]{2,1,0:T(8,128)(2,1)S(1)}, bf16[1,200,768]{2,1,0:T(8,128)(2,1)S(1)}, u32[]{:S(2)}, u32[]{:S(2)}) collective-permute-start(bf16[1,200,768]{2,1,0:T(8,128)(2,1)S(1)} %slice.88), channel_id=1, source_target_pairs={{0,24},{8,0},{16,8},{24,16},{1,25},{9,1},{17,9},{25,17},{2,26},{10... | collective-permute-start | bytes 921608 | tf_op jit(solution)/shard_map/ppermute | solution.py:388
  38.2 18.8 %collective-permute-start.4 = (bf16[1,200,768]{2,1,0:T(8,128)(2,1)S(1)}, bf16[1,200,768]{2,1,0:T(8,128)(2,1)S(1)}, u32[]{:S(2)}, u32[]{:S(2)}) collective-permute-start(bf16[1,200,768]{2,1,0:T(8,128)(2,1)S(1)} %slice.85), channel_id=1, source_target_pairs={{0,2},{2,4},{4,6},{6,0},{1,3},{3,5},{5,7},{7,1},{8,10},{10,12},{12... | collective-permute-start | bytes 921608 | tf_op jit(solution)/shard_map/ppermute | solution.py:388
  53.4 8.4 %collective-permute-start.5 = (bf16[1,200,768]{2,1,0:T(8,128)(2,1)S(1)}, bf16[1,200,768]{2,1,0:T(8,128)(2,1)S(1)}, u32[]{:S(2)}, u32[]{:S(2)}) collective-permute-start(bf16[1,200,768]{2,1,0:T(8,128)(2,1)S(1)} %slice.86), channel_id=1, source_target_pairs={{0,6},{2,0},{4,2},{6,4},{1,7},{3,1},{5,3},{7,5},{8,14},{10,8},{12,... | collective-permute-start | bytes 921608 | tf_op jit(solution)/shard_map/ppermute | solution.py:388
  55.9 7.2 %collective-permute-start = (bf16[4,32,768]{2,0,1:T(4,128)(2,1)S(1)}, bf16[4,32,768]{2,0,1:T(4,128)(2,1)S(1)}, u32[]{:S(2)}, u32[]{:S(2)}) collective-permute-start(bf16[4,32,768]{2,0,1:T(4,128)(2,1)S(1)} %fusion.7), channel_id=1, source_target_pairs={{0,1},{1,0},{2,3},{3,2},{4,5},{5,4},{6,7},{7,6},{8,9},{9,8},{10,11... | collective-permute-start | bytes 589832 | tf_op jit(solution)/shard_map/ppermute | solution.py:403
  57.1 32.2 %collective-permute-start.12 = (bf16[4,200,768]{2,1,0:T(8,128)(2,1)}, bf16[4,200,768]{2,1,0:T(8,128)(2,1)}, u32[]{:S(2)}, u32[]{:S(2)}) collective-permute-start(bf16[4,200,768]{2,1,0:T(8,128)(2,1)} %constant_dynamic-update-slice_fusion.3.rest_5_), channel_id=1, source_target_pairs={{0,6},{2,0},{4,2},{6,4},{1,7},{3,1},{5,3},{7,5},{8,14},{10,8},{12,... | collective-permute-start | bytes 3686408 | tf_op jit(solution)/shard_map/ppermute | solution.py:388
  62.5 31.4 %collective-permute-start.6 = (bf16[4,200,768]{2,1,0:T(8,128)(2,1)}, bf16[4,200,768]{2,1,0:T(8,128)(2,1)}, u32[]{:S(2)}, u32[]{:S(2)}) collective-permute-start(bf16[4,200,768]{2,1,0:T(8,128)(2,1)} %constant_dynamic-update-slice_fusion.rest_1_), channel_id=1, source_target_pairs={{0,24},{8,0},{16,8},{24,16},{1,25},{9,1},{17,9},{25,17},{2,26},{10... | collective-permute-start | bytes 3686408 | tf_op jit(solution)/shard_map/ppermute | solution.py:388
  63.1 53.8 %collective-permute-start.14 = (bf16[4,200,768]{2,1,0:T(8,128)(2,1)S(1)}, bf16[4,200,768]{2,1,0:T(8,128)(2,1)}, u32[]{:S(2)}, u32[]{:S(2)}) collective-permute-start(bf16[4,200,768]{2,1,0:T(8,128)(2,1)S(1)} %pad_maximum_fusion.rest_0_), channel_id=1, source_target_pairs={{0,24},{8,0},{16,8},{24,16},{1,25},{9,1},{17,9},{25,17},{2,26},{10... | collective-permute-start | bytes 3686408 | tf_op jit(solution)/shard_map/ppermute | solution.py:388
  63.2 53.7 %collective-permute-start.16 = (bf16[4,200,768]{2,1,0:T(8,128)(2,1)}, bf16[4,200,768]{2,1,0:T(8,128)(2,1)}, u32[]{:S(2)}, u32[]{:S(2)}) collective-permute-start(bf16[4,200,768]{2,1,0:T(8,128)(2,1)} %pad_maximum_fusion.1.rest_4_), channel_id=1, source_target_pairs={{0,6},{2,0},{4,2},{6,4},{1,7},{3,1},{5,3},{7,5},{8,14},{10,8},{12,... | collective-permute-start | bytes 3686408 | tf_op jit(solution)/shard_map/ppermute | solution.py:388
  65.1 53.9 %collective-permute-start.13 = (bf16[4,200,768]{2,1,0:T(8,128)(2,1)}, bf16[4,200,768]{2,1,0:T(8,128)(2,1)}, u32[]{:S(2)}, u32[]{:S(2)}) collective-permute-start(bf16[4,200,768]{2,1,0:T(8,128)(2,1)} %constant_dynamic-update-slice_fusion.rest_1_), channel_id=1, source_target_pairs={{0,8},{8,16},{16,24},{24,0},{1,9},{9,17},{17,25},{25,1},{2,10},{10... | collective-permute-start | bytes 3686408 | tf_op jit(solution)/shard_map/ppermute | solution.py:388
  89.2 50.9 %collective-permute-start.15 = (bf16[4,200,768]{2,1,0:T(8,128)(2,1)}, bf16[4,200,768]{2,1,0:T(8,128)(2,1)}, u32[]{:S(2)}, u32[]{:S(2)}) collective-permute-start(bf16[4,200,768]{2,1,0:T(8,128)(2,1)} %constant_dynamic-update-slice_fusion.3.rest_5_), channel_id=1, source_target_pairs={{0,2},{2,4},{4,6},{6,0},{1,3},{3,5},{5,7},{7,1},{8,10},{10,12},{12... | collective-permute-start | bytes 3686408 | tf_op jit(solution)/shard_map/ppermute | solution.py:388
  94.0 56.9 %collective-permute-start.17 = (bf16[4,200,768]{2,1,0:T(8,128)(2,1)}, bf16[4,200,768]{2,1,0:T(8,128)(2,1)S(1)}, u32[]{:S(2)}, u32[]{:S(2)}) collective-permute-start(bf16[4,200,768]{2,1,0:T(8,128)(2,1)} %collective-permute-done.2.rest_2_), channel_id=1, source_target_pairs={{0,8},{8,16},{16,24},{24,0},{1,9},{9,17},{17,25},{25,1},{2,10},{10... | collective-permute-start | bytes 3686408 | tf_op jit(solution)/shard_map/ppermute | solution.py:388
  116.9 34.0 %collective-permute-start.18 = (bf16[4,200,768]{2,1,0:T(8,128)(2,1)}, bf16[4,200,768]{2,1,0:T(8,128)(2,1)S(1)}, u32[]{:S(2)}, u32[]{:S(2)}) collective-permute-start(bf16[4,200,768]{2,1,0:T(8,128)(2,1)} %collective-permute-done.6.rest_3_), channel_id=1, source_target_pairs={{0,24},{8,0},{16,8},{24,16},{1,25},{9,1},{17,9},{25,17},{2,26},{10... | collective-permute-start | bytes 3686408 | tf_op jit(solution)/shard_map/ppermute | solution.py:388
  116.9 34.0 %collective-permute-start.19 = (bf16[4,200,768]{2,1,0:T(8,128)(2,1)}, bf16[4,200,768]{2,1,0:T(8,128)(2,1)}, u32[]{:S(2)}, u32[]{:S(2)}) collective-permute-start(bf16[4,200,768]{2,1,0:T(8,128)(2,1)} %collective-permute-done.8.rest_6_), channel_id=1, source_target_pairs={{0,2},{2,4},{4,6},{6,0},{1,3},{3,5},{5,7},{7,1},{8,10},{10,12},{12... | collective-permute-start | bytes 3686408 | tf_op jit(solution)/shard_map/ppermute | solution.py:388
  119.0 31.9 %collective-permute-start.20 = (bf16[4,200,768]{2,1,0:T(8,128)(2,1)}, bf16[4,200,768]{2,1,0:T(8,128)(2,1)}, u32[]{:S(2)}, u32[]{:S(2)}) collective-permute-start(bf16[4,200,768]{2,1,0:T(8,128)(2,1)} %collective-permute-done.12.rest_7_), channel_id=1, source_target_pairs={{0,6},{2,0},{4,2},{6,4},{1,7},{3,1},{5,3},{7,5},{8,14},{10,8},{12,... | collective-permute-start | bytes 3686408 | tf_op jit(solution)/shard_map/ppermute | solution.py:388
  172.0 4.8 %collective-permute-start.21 = (f32[768,768]{1,0:T(8,128)}, f32[768,768]{1,0:T(8,128)S(1)}, u32[]{:S(2)}, u32[]{:S(2)}) collective-permute-start(f32[768,768]{1,0:T(8,128)} %get-tuple-element.61), channel_id=1, source_target_pairs={{0,1},{1,0},{2,3},{3,2},{4,5},{5,4},{6,7},{7,6},{8,9},{9,8},{10,11... | collective-permute-start | bytes 7077896 | tf_op jit(solution)/shard_map/ppermute | solution.py:403
  172.1 6.7 %collective-permute-start.22 = (f32[136,768]{1,0:T(8,128)}, f32[136,768]{1,0:T(8,128)S(1)}, u32[]{:S(2)}, u32[]{:S(2)}) collective-permute-start(f32[136,768]{1,0:T(8,128)} %get-tuple-element.62), channel_id=1, source_target_pairs={{0,1},{1,0},{2,3},{3,2},{4,5},{5,4},{6,7},{7,6},{8,9},{9,8},{10,11... | collective-permute-start | bytes 1253384 | tf_op jit(solution)/shard_map/ppermute | solution.py:403
  182.9 28.4 %collective-permute-start.26 = (f32[384,768]{1,0:T(8,128)}, f32[384,768]{1,0:T(8,128)}, u32[]{:S(2)}, u32[]{:S(2)}) collective-permute-start(f32[384,768]{1,0:T(8,128)} %get-tuple-element.70), channel_id=1, source_target_pairs={{0,1},{1,0},{2,3},{3,2},{4,5},{5,4},{6,7},{7,6},{8,9},{9,8},{10,11... | collective-permute-start | bytes 3538952 | tf_op jit(solution)/shard_map/ppermute | solution.py:403
  184.1 16.8 %collective-permute-start.23 = (f32[96,768]{1,0:T(8,128)}, f32[96,768]{1,0:T(8,128)}, u32[]{:S(2)}, u32[]{:S(2)}) collective-permute-start(f32[96,768]{1,0:T(8,128)} %get-tuple-element.83), channel_id=1, source_target_pairs={{0,2},{2,4},{4,6},{6,0},{1,3},{3,5},{5,7},{7,1},{8,10},{10,12},{12... | collective-permute-start | bytes 884744 | tf_op jit(solution)/shard_map/ppermute | solution.py:442
  184.1 18.9 %collective-permute-start.24 = (f32[96,768]{1,0:T(8,128)}, f32[96,768]{1,0:T(8,128)}, u32[]{:S(2)}, u32[]{:S(2)}) collective-permute-start(f32[96,768]{1,0:T(8,128)} %get-tuple-element.85), channel_id=1, source_target_pairs={{0,4},{2,6},{4,0},{6,2},{1,5},{3,7},{5,1},{7,3},{8,12},{10,14},{12... | collective-permute-start | bytes 884744 | tf_op jit(solution)/shard_map/ppermute | solution.py:442
  194.8 13.7 %collective-permute-start.25 = (f32[96,768]{1,0:T(8,128)}, f32[96,768]{1,0:T(8,128)}, u32[]{:S(2)}, u32[]{:S(2)}) collective-permute-start(f32[96,768]{1,0:T(8,128)} %get-tuple-element.84), channel_id=1, source_target_pairs={{0,6},{2,0},{4,2},{6,4},{1,7},{3,1},{5,3},{7,5},{8,14},{10,8},{12,... | collective-permute-start | bytes 884744 | tf_op jit(solution)/shard_map/ppermute | solution.py:442
  196.0 14.4 %copy-start.12 = (f32[16,256]{1,0:T(8,128)S(1)}, f32[16,256]{1,0:T(8,128)}, u32[]{:S(2)}) copy-start(f32[16,256]{1,0:T(8,128)} %get-tuple-element.66) | copy-start | bytes 49156
  196.0 15.3 %copy-start.6 = (f32[384,768]{1,0:T(8,128)S(1)}, f32[384,768]{1,0:T(8,128)}, u32[]{:S(2)}) copy-start(f32[384,768]{1,0:T(8,128)} %get-tuple-element.69) | copy-start | bytes 3538948
  196.0 28.6 %collective-permute-start.30 = (f32[96,768]{1,0:T(8,128)}, f32[96,768]{1,0:T(8,128)}, u32[]{:S(2)}, u32[]{:S(2)}) collective-permute-start(f32[96,768]{1,0:T(8,128)} %get-tuple-element.77), channel_id=1, source_target_pairs={{0,8},{8,16},{16,24},{24,0},{1,9},{9,17},{17,25},{25,1},{2,10},{10... | collective-permute-start | bytes 884744 | tf_op jit(solution)/shard_map/ppermute | solution.py:442
  200.9 24.4 %collective-permute-start.31 = (f32[96,768]{1,0:T(8,128)}, f32[96,768]{1,0:T(8,128)}, u32[]{:S(2)}, u32[]{:S(2)}) collective-permute-start(f32[96,768]{1,0:T(8,128)} %get-tuple-element.79), channel_id=1, source_target_pairs={{0,16},{8,24},{16,0},{24,8},{1,17},{9,25},{17,1},{25,9},{2,18},{10... | collective-permute-start | bytes 884744 | tf_op jit(solution)/shard_map/ppermute | solution.py:442
  203.0 24.9 %collective-permute-start.32 = (f32[96,768]{1,0:T(8,128)}, f32[96,768]{1,0:T(8,128)}, u32[]{:S(2)}, u32[]{:S(2)}) collective-permute-start(f32[96,768]{1,0:T(8,128)} %get-tuple-element.78), channel_id=1, source_target_pairs={{0,24},{8,0},{16,8},{24,16},{1,25},{9,1},{17,9},{25,17},{2,26},{10... | collective-permute-start | bytes 884744 | tf_op jit(solution)/shard_map/ppermute | solution.py:442
  212.8 17.9 %collective-permute-start.27 = (f32[96,768]{1,0:T(8,128)S(1)}, f32[96,768]{1,0:T(8,128)S(1)}, u32[]{:S(2)}, u32[]{:S(2)}) collective-permute-start(f32[96,768]{1,0:T(8,128)S(1)} %get-tuple-element.80), channel_id=1, source_target_pairs={{0,32},{32,64},{64,96},{96,0},{1,33},{33,65},{65,97},{97,1},{2,34}... | collective-permute-start | bytes 884744 | tf_op jit(solution)/shard_map/ppermute | solution.py:442
  219.5 13.1 %collective-permute-start.28 = (f32[96,768]{1,0:T(8,128)S(1)}, f32[96,768]{1,0:T(8,128)S(1)}, u32[]{:S(2)}, u32[]{:S(2)}) collective-permute-start(f32[96,768]{1,0:T(8,128)S(1)} %get-tuple-element.82), channel_id=1, source_target_pairs={{0,64},{32,96},{64,0},{96,32},{1,65},{33,97},{65,1},{97,33},{2,66}... | collective-permute-start | bytes 884744 | tf_op jit(solution)/shard_map/ppermute | solution.py:442
  224.6 12.4 %collective-permute-start.29 = (f32[96,768]{1,0:T(8,128)S(1)}, f32[96,768]{1,0:T(8,128)S(1)}, u32[]{:S(2)}, u32[]{:S(2)}) collective-permute-start(f32[96,768]{1,0:T(8,128)S(1)} %get-tuple-element.81), channel_id=1, source_target_pairs={{0,96},{32,0},{64,32},{96,64},{1,97},{33,1},{65,33},{97,65},{2,98}... | collective-permute-start | bytes 884744 | tf_op jit(solution)/shard_map/ppermute | solution.py:442
  225.3 17.1 %collective-permute-start.39 = (f32[24,768]{1,0:T(8,128)S(1)}, f32[24,768]{1,0:T(8,128)S(1)}, u32[]{:S(2)}, u32[]{:S(2)}) collective-permute-start(f32[24,768]{1,0:T(8,128)S(1)} %get-tuple-element.89), channel_id=1, source_target_pairs={{0,8},{8,16},{16,24},{24,0},{1,9},{9,17},{17,25},{25,1},{2,10},{10... | collective-permute-start | bytes 221192 | tf_op jit(solution)/shard_map/ppermute | solution.py:442
  228.0 14.5 %collective-permute-start.40 = (f32[24,768]{1,0:T(8,128)S(1)}, f32[24,768]{1,0:T(8,128)S(1)}, u32[]{:S(2)}, u32[]{:S(2)}) collective-permute-start(f32[24,768]{1,0:T(8,128)S(1)} %get-tuple-element.91), channel_id=1, source_target_pairs={{0,16},{8,24},{16,0},{24,8},{1,17},{9,25},{17,1},{25,9},{2,18},{10... | collective-permute-start | bytes 221192 | tf_op jit(solution)/shard_map/ppermute | solution.py:442
  230.7 11.7 %collective-permute-start.41 = (f32[24,768]{1,0:T(8,128)S(1)}, f32[24,768]{1,0:T(8,128)S(1)}, u32[]{:S(2)}, u32[]{:S(2)}) collective-permute-start(f32[24,768]{1,0:T(8,128)S(1)} %get-tuple-element.90), channel_id=1, source_target_pairs={{0,24},{8,0},{16,8},{24,16},{1,25},{9,1},{17,9},{25,17},{2,26},{10... | collective-permute-start | bytes 221192 | tf_op jit(solution)/shard_map/ppermute | solution.py:442
  237.2 7.8 %collective-permute-start.33 = (f32[48,768]{1,0:T(8,128)S(1)}, f32[48,768]{1,0:T(8,128)S(1)}, u32[]{:S(2)}, u32[]{:S(2)}) collective-permute-start(f32[48,768]{1,0:T(8,128)S(1)} %get-tuple-element.86), channel_id=1, source_target_pairs={{0,2},{2,4},{4,6},{6,0},{1,3},{3,5},{5,7},{7,1},{8,10},{10,12},{12... | collective-permute-start | bytes 442376 | tf_op jit(solution)/shard_map/ppermute | solution.py:442
  239.7 8.2 %collective-permute-start.34 = (f32[48,768]{1,0:T(8,128)S(1)}, f32[48,768]{1,0:T(8,128)S(1)}, u32[]{:S(2)}, u32[]{:S(2)}) collective-permute-start(f32[48,768]{1,0:T(8,128)S(1)} %get-tuple-element.87), channel_id=1, source_target_pairs={{0,4},{2,6},{4,0},{6,2},{1,5},{3,7},{5,1},{7,3},{8,12},{10,14},{12... | collective-permute-start | bytes 442376 | tf_op jit(solution)/shard_map/ppermute | solution.py:442
  242.4 7.4 %collective-permute-start.35 = (f32[48,768]{1,0:T(8,128)S(1)}, f32[48,768]{1,0:T(8,128)S(1)}, u32[]{:S(2)}, u32[]{:S(2)}) collective-permute-start(f32[48,768]{1,0:T(8,128)S(1)} %get-tuple-element.88), channel_id=1, source_target_pairs={{0,6},{2,0},{4,2},{6,4},{1,7},{3,1},{5,3},{7,5},{8,14},{10,8},{12,... | collective-permute-start | bytes 442376 | tf_op jit(solution)/shard_map/ppermute | solution.py:442
  249.9 6.1 %collective-permute-start.36 = (f32[6,768]{1,0:T(8,128)S(1)}, f32[6,768]{1,0:T(8,128)S(1)}, u32[]{:S(2)}, u32[]{:S(2)}) collective-permute-start(f32[6,768]{1,0:T(8,128)S(1)} %get-tuple-element.97), channel_id=1, source_target_pairs={{0,8},{8,16},{16,24},{24,0},{1,9},{9,17},{17,25},{25,1},{2,10},{10... | collective-permute-start | bytes 55304 | tf_op jit(solution)/shard_map/ppermute | solution.py:442
  251.3 5.3 %collective-permute-start.37 = (f32[6,768]{1,0:T(8,128)S(1)}, f32[6,768]{1,0:T(8,128)S(1)}, u32[]{:S(2)}, u32[]{:S(2)}) collective-permute-start(f32[6,768]{1,0:T(8,128)S(1)} %get-tuple-element.99), channel_id=1, source_target_pairs={{0,16},{8,24},{16,0},{24,8},{1,17},{9,25},{17,1},{25,9},{2,18},{10... | collective-permute-start | bytes 55304 | tf_op jit(solution)/shard_map/ppermute | solution.py:442
  253.3 5.0 %collective-permute-start.38 = (f32[6,768]{1,0:T(8,128)S(1)}, f32[6,768]{1,0:T(8,128)S(1)}, u32[]{:S(2)}, u32[]{:S(2)}) collective-permute-start(f32[6,768]{1,0:T(8,128)S(1)} %get-tuple-element.98), channel_id=1, source_target_pairs={{0,24},{8,0},{16,8},{24,16},{1,25},{9,1},{17,9},{25,17},{2,26},{10... | collective-permute-start | bytes 55304 | tf_op jit(solution)/shard_map/ppermute | solution.py:442
  253.5 5.5 %collective-permute-start.42 = (f32[12,768]{1,0:T(8,128)S(1)}, f32[12,768]{1,0:T(8,128)S(1)}, u32[]{:S(2)}, u32[]{:S(2)}) collective-permute-start(f32[12,768]{1,0:T(8,128)S(1)} %get-tuple-element.92), channel_id=1, source_target_pairs={{0,32},{32,64},{64,96},{96,0},{1,33},{33,65},{65,97},{97,1},{2,34}... | collective-permute-start | bytes 110600 | tf_op jit(solution)/shard_map/ppermute | solution.py:442
  253.6 6.0 %collective-permute-start.43 = (f32[12,768]{1,0:T(8,128)S(1)}, f32[12,768]{1,0:T(8,128)S(1)}, u32[]{:S(2)}, u32[]{:S(2)}) collective-permute-start(f32[12,768]{1,0:T(8,128)S(1)} %get-tuple-element.93), channel_id=1, source_target_pairs={{0,64},{32,96},{64,0},{96,32},{1,65},{33,97},{65,1},{97,33},{2,66}... | collective-permute-start | bytes 110600 | tf_op jit(solution)/shard_map/ppermute | solution.py:442
  256.0 5.3 %collective-permute-start.44 = (f32[12,768]{1,0:T(8,128)S(1)}, f32[12,768]{1,0:T(8,128)S(1)}, u32[]{:S(2)}, u32[]{:S(2)}) collective-permute-start(f32[12,768]{1,0:T(8,128)S(1)} %get-tuple-element.94), channel_id=1, source_target_pairs={{0,96},{32,0},{64,32},{96,64},{1,97},{33,1},{65,33},{97,65},{2,98}... | collective-permute-start | bytes 110600 | tf_op jit(solution)/shard_map/ppermute | solution.py:442
  (12 other events, 61.6 us)

commit v2 on v1

--- a/solution.py
+++ b/solution.py
@@ -502,12 +502,9 @@
     )
     got = swapped(give)
     from_core = swapped(other)
+    mine_query, other_query = query_gradient(spot, text, dq, got, rings)
     rest = mine.shape[0] // 2
-    key_part, value_part, got = lax.optimization_barrier(
-        (mine[:rest] + from_core[:rest], mine[rest:] + from_core[rest:], got)
-    )
-    mine_query, other_query = query_gradient(spot, text, dq, got, rings)
-    parts = [mine_query + swapped(other_query), key_part, value_part]
+    parts = [mine_query + swapped(other_query), mine[:rest] + from_core[:rest], mine[rest:] + from_core[rest:]]
     (grad_query, grad_key, grad_value), (rows, got) = reduce_gradients(parts, (rows, got))
     half = picks.shape[0] // 2
     rows = rows[:half] + got[pairs * QP :, :GW]

time: 267 us -> 266 us (level)
  starting transfers between devices: 65.5 us -> 83.2 us
  waiting for transfers between devices: 89.6 us -> 77.9 us
  other arithmetic: 13.2 us -> 8.59 us
    ppermute x21, starting transfers between devices: 41.1 us -> 58.6 us  [ring_scatter(): lax.ppermute(piece, axis, [(k, (k + step) % n) for k in range(n)])]
    ppermute x21, waiting for transfers between devices: 26.8 us -> 11.8 us  [ring_scatter(): lax.ppermute(piece, axis, [(k, (k + step) % n) for k in range(n)])]
    ppermute x4, waiting for transfers between devices: 4.24 us -> 7.53 us  [swapped(): return lax.ppermute(x, 'dev_2', [(0, 1), (1, 0)])]
    add x7, other arithmetic: 4.08 us -> 0.92 us  [reduce_gradients(): kept = kept + piece]
    unnamed x37 -> x35, local copies, waits for them, and re-layouts: 9.81 us -> 9.15 us
  transfers between devices with their start and end apart: 45 -> 45, of which waited for: 20 -> 17; matrix products, arithmetic and copies ran while one was open for 12% -> 9% of each run, Pallas kernels for 18% -> 19%
where the time goes in v2:
time: 266 us; the launch traced here: 261 us
  starting transfers between devices  83.2 us (31%)
  waiting for transfers between devices  77.9 us (29%)
  Pallas kernels  69.5 us (26%)
  local copies, waits for them, and re-layouts  20.7 us (8%)
  other arithmetic  8.59 us (3%)
    ppermute x21, starting transfers between devices, ring_scatter(): lax.ppermute(piece, axis, [(k, (k + step) % n) for k in range(n)])  58.6 us
    ppermute x20, waiting for transfers between devices, shift(): return lax.ppermute(x, axis, [(k, (k + step) % n) for k in range(n)])  58.6 us
    pallas_call x3, Pallas kernels, negative_pairs(): pl.pallas_call(functools.partial(negatives_kernel, pairs=pairs, rings=rin...  48.9 us
    ppermute x20, starting transfers between devices, shift(): return lax.ppermute(x, axis, [(k, (k + step) % n) for k in range(n)])  23.6 us
    pallas_call x1, Pallas kernels, own_pairs(): pl.pallas_call(functools.partial(own_kernel, pairs=pairs), name='own_pair...  17.2 us
    ppermute x21, waiting for transfers between devices, ring_scatter(): lax.ppermute(piece, axis, [(k, (k + step) % n) for k in range(n)])  11.8 us
    unnamed x35, local copies, waits for them, and re-layouts  9.15 us
    ppermute x4, waiting for transfers between devices, swapped(): return lax.ppermute(x, 'dev_2', [(0, 1), (1, 0)])  7.53 us
  transfers between devices with their start and end apart: 45, of which 17 were waited for; matrix products, arithmetic and copies ran while one was open for 9% of the time, Pallas kernels for 19%

profile of v2, /device:TPU:110, one launch (start us, length us, event | category | flops | bytes accessed | tf_op | source)
XLA Modules:
  0.0 261.0 jit_solution(9277153119630533194)
XLA Ops:
  0.6 1.4 copy.32
  3.0 1.6 collective-permute-start.1
  4.5 2.0 collective-permute-start.9
  6.6 12.0 %collective-permute-done.1 = bf16[2,200,768]{2,1,0:T(8,128)(2,1)S(1)} collective-permute-done((bf16[2,200,768]{2,1,0:T(8,128)(2,1)S(1)}, bf16[2,200,768]{2,1,0:T(8,128)(2,1)S(1)}, u32[]{:S(2)}, u32[]{:S(2)}) %collective-permute-start.1) | collective-permute-done | bytes 614432 | tf_op jit(solution)/shard_map/ppermute | solution.py:388
  18.8 1.3 collective-permute-done.7
  20.1 2.5 pad_maximum_fusion.1.rest_4_
  22.5 1.3 collective-permute-start.8
  25.7 1.6 collective-permute-start.10
  29.0 1.9 constant_dynamic-update-slice_fusion.5
  31.0 7.2 %collective-permute-done.3 = bf16[2,200,768]{2,1,0:T(8,128)(2,1)} collective-permute-done((bf16[2,200,768]{2,1,0:T(8,128)(2,1)S(1)}, bf16[2,200,768]{2,1,0:T(8,128)(2,1)}, u32[]{:S(2)}, u32[]{:S(2)}) %collective-permute-start.3) | collective-permute-done | bytes 614432 | tf_op jit(solution)/shard_map/ppermute | solution.py:388
  38.2 1.1 collective-permute-start.4
  40.3 1.9 constant_dynamic-update-slice_fusion.2
  42.3 11.1 %collective-permute-done.10 = bf16[1,200,768]{2,1,0:T(8,128)(2,1)S(1)} collective-permute-done((bf16[1,200,768]{2,1,0:T(8,128)(2,1)S(1)}, bf16[1,200,768]{2,1,0:T(8,128)(2,1)S(1)}, u32[]{:S(2)}, u32[]{:S(2)}) %collective-permute-start.10) | collective-permute-done | bytes 307232 | tf_op jit(solution)/shard_map/ppermute | solution.py:388
  53.4 1.8 collective-permute-start.5
  57.1 2.5 collective-permute-start.12
  60.4 1.4 collective-permute-done.5
  63.2 1.9 collective-permute-start.16
  65.1 3.1 %collective-permute-start.13 = (bf16[4,200,768]{2,1,0:T(8,128)(2,1)}, bf16[4,200,768]{2,1,0:T(8,128)(2,1)}, u32[]{:S(2)}, u32[]{:S(2)}) collective-permute-start(bf16[4,200,768]{2,1,0:T(8,128)(2,1)} %constant_dynamic-update-slice_fusion.rest_1_), channel_id=1, source_target_pairs={{0,8},{8,16},{16,24},{24,0},{1,9},{9,17},{17,25},{25,1},{2,10},{10... | collective-permute-start | bytes 3686408 | tf_op jit(solution)/shard_map/ppermute | solution.py:388
  68.9 1.2 pad.14.image_ref
  72.1 17.2 %own_pairs.1 = (bf16[24,128,256]{2,1,0:T(8,128)(2,1)}, bf16[9,128,256]{2,1,0:T(8,128)(2,1)}, bf16[128,256]{1,0:T(8,128)(2,1)}, f32[768,1536]{1,0:T(8,128)}, f32[256,768]{1,0:T(8,128)}, /*index=5*/f32[4,256]{1,0:T(4,128)}) custom-call(f32[4]{0:T(128)} %slice_reduce_fusion.tan_ref, bf16[128,768]{1,0:T(8,128)(2,1)} %bitcast.115, bf16[128,768]{1,0:T(8,128)(2,1)} %bitcast.119, ...), custom_call_target="tpu_custom_call" | custom-call | tf_op jit(solution)/shard_map/own_pairs/pallas_call | solution.py:306
  89.3 1.8 collective-permute-start.15
  91.1 2.8 %collective-permute-done.6.rest_3_ = bf16[4,200,768]{2,1,0:T(8,128)(2,1)} collective-permute-done((bf16[4,200,768]{2,1,0:T(8,128)(2,1)}, bf16[4,200,768]{2,1,0:T(8,128)(2,1)}, u32[]{:S(2)}, u32[]{:S(2)}) %collective-permute-start.6) | collective-permute-done | bytes 1228832 | tf_op jit(solution)/shard_map/ppermute | solution.py:388
  94.6 22.3 %collective-permute-done.14.rest_1_ = bf16[4,200,768]{2,1,0:T(8,128)(2,1)} collective-permute-done((bf16[4,200,768]{2,1,0:T(8,128)(2,1)S(1)}, bf16[4,200,768]{2,1,0:T(8,128)(2,1)}, u32[]{:S(2)}, u32[]{:S(2)}) %collective-permute-start.14) | collective-permute-done | bytes 1228832 | tf_op jit(solution)/shard_map/ppermute | solution.py:388
  116.9 2.1 collective-permute-start.19
  121.6 18.6 %shard_map.94 = (f32[768,1536]{1,0:T(8,128)}, f32[256,768]{1,0:T(8,128)}, f32[16,256]{1,0:T(8,128)}) custom-call(s32[16]{0:T(128)} %reshape.54.pick_ref, f32[16]{0:T(128)} %reshape.55.tan_ref, s32[3]{0:T(128)} %pad_add_fusion.1.spot_ref, bf16[24,128,256]{2,1,0:T(8,128)(2,1)} %get-tuple-element.36.qx_ref, bf16[9,128,256]{2,1,0:T(8,128)(2,1)} %get-tuple-element.37.mhx_ref, ...), custom_call_target="tpu_custom_call" | custom-call | tf_op jit(solution)/shard_map/pallas_call | solution.py:348
  140.2 10.7 %shard_map.95 = (f32[768,1536]{1,0:T(8,128)}, f32[256,768]{1,0:T(8,128)}, f32[16,256]{1,0:T(8,128)}) custom-call(s32[16]{0:T(128)} %reshape.54.pick_ref, f32[16]{0:T(128)} %reshape.55.tan_ref, s32[3]{0:T(128)} %pad_add_fusion.1.spot_ref, bf16[24,128,256]{2,1,0:T(8,128)(2,1)} %get-tuple-element.36.qx_ref, bf16[9,128,256]{2,1,0:T(8,128)(2,1)} %get-tuple-element.37.mhx_ref, ...), custom_call_target="tpu_custom_call" | custom-call | tf_op jit(solution)/shard_map/pallas_call | solution.py:348
  152.3 19.7 %shard_map.96 = (f32[768,768]{1,0:T(8,128)}, f32[768,768]{1,0:T(8,128)}, f32[128,768]{1,0:T(8,128)}, f32[136,768]{1,0:T(8,128)}, f32[16,256]{1,0:T(8,128)}) custom-call(s32[16]{0:T(128)} %reshape.54.pick_ref, f32[16]{0:T(128)} %reshape.55.tan_ref, s32[3]{0:T(128)} %pad_add_fusion.1.spot_ref, bf16[24,128,256]{2,1,0:T(8,128)(2,1)} %get-tuple-element.36.qx_ref, ...), custom_call_target="tpu_custom_call" | custom-call | tf_op jit(solution)/shard_map/pallas_call | solution.py:348
  172.6 4.8 %collective-permute-done.25.got_ref = f32[136,768]{1,0:T(8,128)S(1)} collective-permute-done((f32[136,768]{1,0:T(8,128)}, f32[136,768]{1,0:T(8,128)S(1)}, u32[]{:S(2)}, u32[]{:S(2)}) %collective-permute-start.25) | collective-permute-done | bytes 417824 | tf_op jit(solution)/shard_map/ppermute | solution.py:403
  178.2 3.4 %query_gradient.1 = (f32[384,768]{1,0:T(8,128)}, f32[384,768]{1,0:T(8,128)}) custom-call(s32[3]{0:T(128)} %pad_add_fusion.1.spot_ref, bf16[128,768]{1,0:T(8,128)(2,1)} %bitcast.116, f32[128,768]{1,0:T(8,128)} %get-tuple-element.63.dq_ref, f32[136,768]{1,0:T(8,128)} %copy-done.8), custom_call_target="tpu_custom_call" | custom-call | tf_op jit(solution)/shard_map/query_gradient/pallas_call | solution.py:371
  182.3 2.7 %collective-permute-done.26 = f32[384,768]{1,0:T(8,128)S(1)} collective-permute-done((f32[384,768]{1,0:T(8,128)}, f32[384,768]{1,0:T(8,128)S(1)}, u32[]{:S(2)}, u32[]{:S(2)}) %collective-permute-start.26) | collective-permute-done | bytes 1179680 | tf_op jit(solution)/shard_map/ppermute | solution.py:403
  185.0 1.6 add.232
  187.6 4.1 %collective-permute-start.28 = (f32[96,768]{1,0:T(8,128)S(1)}, f32[96,768]{1,0:T(8,128)S(1)}, u32[]{:S(2)}, u32[]{:S(2)}) collective-permute-start(f32[96,768]{1,0:T(8,128)S(1)} %get-tuple-element.76), channel_id=1, source_target_pairs={{0,64},{32,96},{64,0},{96,32},{1,65},{33,97},{65,1},{97,33},{2,66}... | collective-permute-start | bytes 884744 | tf_op jit(solution)/shard_map/ppermute | solution.py:442
  192.1 9.5 %collective-permute-start.22 = (f32[96,768]{1,0:T(8,128)S(1)}, f32[96,768]{1,0:T(8,128)S(1)}, u32[]{:S(2)}, u32[]{:S(2)}) collective-permute-start(f32[96,768]{1,0:T(8,128)S(1)} %get-tuple-element.77), channel_id=1, source_target_pairs={{0,2},{2,4},{4,6},{6,0},{1,3},{3,5},{5,7},{7,1},{8,10},{10,12},{12... | collective-permute-start | bytes 884744 | tf_op jit(solution)/shard_map/ppermute | solution.py:442
  201.6 5.7 %collective-permute-start.23 = (f32[96,768]{1,0:T(8,128)S(1)}, f32[96,768]{1,0:T(8,128)S(1)}, u32[]{:S(2)}, u32[]{:S(2)}) collective-permute-start(f32[96,768]{1,0:T(8,128)S(1)} %get-tuple-element.79), channel_id=1, source_target_pairs={{0,4},{2,6},{4,0},{6,2},{1,5},{3,7},{5,1},{7,3},{8,12},{10,14},{12... | collective-permute-start | bytes 884744 | tf_op jit(solution)/shard_map/ppermute | solution.py:442
  207.3 6.9 %collective-permute-start.24 = (f32[96,768]{1,0:T(8,128)S(1)}, f32[96,768]{1,0:T(8,128)S(1)}, u32[]{:S(2)}, u32[]{:S(2)}) collective-permute-start(f32[96,768]{1,0:T(8,128)S(1)} %get-tuple-element.78), channel_id=1, source_target_pairs={{0,6},{2,0},{4,2},{6,4},{1,7},{3,1},{5,3},{7,5},{8,14},{10,8},{12,... | collective-permute-start | bytes 884744 | tf_op jit(solution)/shard_map/ppermute | solution.py:442
  214.4 1.5 collective-permute-start.31
  215.9 6.3 %collective-permute-start.32 = (f32[96,768]{1,0:T(8,128)S(1)}, f32[96,768]{1,0:T(8,128)S(1)}, u32[]{:S(2)}, u32[]{:S(2)}) collective-permute-start(f32[96,768]{1,0:T(8,128)S(1)} %get-tuple-element.72), channel_id=1, source_target_pairs={{0,24},{8,0},{16,8},{24,16},{1,25},{9,1},{17,9},{25,17},{2,26},{10... | collective-permute-start | bytes 884744 | tf_op jit(solution)/shard_map/ppermute | solution.py:442
  222.9 5.2 %collective-permute-start.40 = (f32[24,768]{1,0:T(8,128)S(1)}, f32[24,768]{1,0:T(8,128)S(1)}, u32[]{:S(2)}, u32[]{:S(2)}) collective-permute-start(f32[24,768]{1,0:T(8,128)S(1)} %get-tuple-element.85), channel_id=1, source_target_pairs={{0,16},{8,24},{16,0},{24,8},{1,17},{9,25},{17,1},{25,9},{2,18},{10... | collective-permute-start | bytes 221192 | tf_op jit(solution)/shard_map/ppermute | solution.py:442
  228.2 2.4 collective-permute-done.32
  230.7 10.1 %collective-permute-start.33 = (f32[48,768]{1,0:T(8,128)S(1)}, f32[48,768]{1,0:T(8,128)S(1)}, u32[]{:S(2)}, u32[]{:S(2)}) collective-permute-start(f32[48,768]{1,0:T(8,128)S(1)} %get-tuple-element.80), channel_id=1, source_target_pairs={{0,2},{2,4},{4,6},{6,0},{1,3},{3,5},{5,7},{7,1},{8,10},{10,12},{12... | collective-permute-start | bytes 442376 | tf_op jit(solution)/shard_map/ppermute | solution.py:442
  242.3 2.2 collective-permute-start.35
  244.5 1.2 collective-permute-done.33
  245.7 2.2 collective-permute-done.34
  247.9 1.5 collective-permute-done.35
  249.6 2.0 collective-permute-start.37
  251.6 2.5 collective-permute-start.42
  255.1 1.4 collective-permute-done.38
  257.2 2.6 collective-permute-done.43
  (135 shorter events, 26.3 us)
Async XLA Ops:
  3.0 15.6 %collective-permute-start.1 = (bf16[2,200,768]{2,1,0:T(8,128)(2,1)S(1)}, bf16[2,200,768]{2,1,0:T(8,128)(2,1)S(1)}, u32[]{:S(2)}, u32[]{:S(2)}) collective-permute-start(bf16[2,200,768]{2,1,0:T(8,128)(2,1)S(1)} %get-tuple-element.70), channel_id=1, source_target_pairs={{0,2},{2,4},{4,6},{6,0},{1,3},{3,5},{5,7},{7,1},{8,10},{10,12},{12... | collective-permute-start | bytes 1843208 | tf_op jit(solution)/shard_map/ppermute | solution.py:388
  4.5 15.5 %collective-permute-start.7 = (bf16[2,200,768]{2,1,0:T(8,128)(2,1)}, bf16[2,200,768]{2,1,0:T(8,128)(2,1)S(1)}, u32[]{:S(2)}, u32[]{:S(2)}) collective-permute-start(bf16[2,200,768]{2,1,0:T(8,128)(2,1)} %get-tuple-element.69), channel_id=1, source_target_pairs={{0,8},{8,16},{16,24},{24,0},{1,9},{9,17},{17,25},{25,1},{2,10},{10... | collective-permute-start | bytes 1843208 | tf_op jit(solution)/shard_map/ppermute | solution.py:388
  4.5 22.9 %collective-permute-start.9 = (bf16[2,200,768]{2,1,0:T(8,128)(2,1)}, bf16[2,200,768]{2,1,0:T(8,128)(2,1)}, u32[]{:S(2)}, u32[]{:S(2)}) collective-permute-start(bf16[2,200,768]{2,1,0:T(8,128)(2,1)} %get-tuple-element.69), channel_id=1, source_target_pairs={{0,24},{8,0},{16,8},{24,16},{1,25},{9,1},{17,9},{25,17},{2,26},{10... | collective-permute-start | bytes 1843208 | tf_op jit(solution)/shard_map/ppermute | solution.py:388
  18.7 44.4 %copy-start = (bf16[4,200,768]{2,1,0:T(8,128)(2,1)}, bf16[4,200,768]{2,1,0:T(8,128)(2,1)S(1)}, u32[]{:S(2)}) copy-start(bf16[4,200,768]{2,1,0:T(8,128)(2,1)S(1)} %pad_maximum_fusion.rest_0_) | copy-start | bytes 3686404
  18.7 44.5 %collective-permute-start.2 = (bf16[4,200,768]{2,1,0:T(8,128)(2,1)S(1)}, bf16[4,200,768]{2,1,0:T(8,128)(2,1)}, u32[]{:S(2)}, u32[]{:S(2)}) collective-permute-start(bf16[4,200,768]{2,1,0:T(8,128)(2,1)S(1)} %pad_maximum_fusion.rest_0_), channel_id=1, source_target_pairs={{0,8},{8,16},{16,24},{24,0},{1,9},{9,17},{17,25},{25,1},{2,10},{10... | collective-permute-start | bytes 3686408 | tf_op jit(solution)/shard_map/ppermute | solution.py:388
  22.5 42.6 %collective-permute-start.8 = (bf16[4,200,768]{2,1,0:T(8,128)(2,1)}, bf16[4,200,768]{2,1,0:T(8,128)(2,1)}, u32[]{:S(2)}, u32[]{:S(2)}) collective-permute-start(bf16[4,200,768]{2,1,0:T(8,128)(2,1)} %pad_maximum_fusion.1.rest_4_), channel_id=1, source_target_pairs={{0,2},{2,4},{4,6},{6,0},{1,3},{3,5},{5,7},{7,1},{8,10},{10,12},{12... | collective-permute-start | bytes 3686408 | tf_op jit(solution)/shard_map/ppermute | solution.py:388
  23.8 14.4 %collective-permute-start.3 = (bf16[2,200,768]{2,1,0:T(8,128)(2,1)S(1)}, bf16[2,200,768]{2,1,0:T(8,128)(2,1)}, u32[]{:S(2)}, u32[]{:S(2)}) collective-permute-start(bf16[2,200,768]{2,1,0:T(8,128)(2,1)S(1)} %get-tuple-element.70), channel_id=1, source_target_pairs={{0,6},{2,0},{4,2},{6,4},{1,7},{3,1},{5,3},{7,5},{8,14},{10,8},{12,... | collective-permute-start | bytes 1843208 | tf_op jit(solution)/shard_map/ppermute | solution.py:388
  25.7 27.6 %collective-permute-start.10 = (bf16[1,200,768]{2,1,0:T(8,128)(2,1)S(1)}, bf16[1,200,768]{2,1,0:T(8,128)(2,1)S(1)}, u32[]{:S(2)}, u32[]{:S(2)}) collective-permute-start(bf16[1,200,768]{2,1,0:T(8,128)(2,1)S(1)} %slice.87), channel_id=1, source_target_pairs={{0,8},{8,16},{16,24},{24,0},{1,9},{9,17},{17,25},{25,1},{2,10},{10... | collective-permute-start | bytes 921608 | tf_op jit(solution)/shard_map/ppermute | solution.py:388
  28.4 27.5 %collective-permute-start.11 = (bf16[1,200,768]{2,1,0:T(8,128)(2,1)S(1)}, bf16[1,200,768]{2,1,0:T(8,128)(2,1)S(1)}, u32[]{:S(2)}, u32[]{:S(2)}) collective-permute-start(bf16[1,200,768]{2,1,0:T(8,128)(2,1)S(1)} %slice.88), channel_id=1, source_target_pairs={{0,24},{8,0},{16,8},{24,16},{1,25},{9,1},{17,9},{25,17},{2,26},{10... | collective-permute-start | bytes 921608 | tf_op jit(solution)/shard_map/ppermute | solution.py:388
  38.2 18.8 %collective-permute-start.4 = (bf16[1,200,768]{2,1,0:T(8,128)(2,1)S(1)}, bf16[1,200,768]{2,1,0:T(8,128)(2,1)S(1)}, u32[]{:S(2)}, u32[]{:S(2)}) collective-permute-start(bf16[1,200,768]{2,1,0:T(8,128)(2,1)S(1)} %slice.85), channel_id=1, source_target_pairs={{0,2},{2,4},{4,6},{6,0},{1,3},{3,5},{5,7},{7,1},{8,10},{10,12},{12... | collective-permute-start | bytes 921608 | tf_op jit(solution)/shard_map/ppermute | solution.py:388
  53.4 8.4 %collective-permute-start.5 = (bf16[1,200,768]{2,1,0:T(8,128)(2,1)S(1)}, bf16[1,200,768]{2,1,0:T(8,128)(2,1)S(1)}, u32[]{:S(2)}, u32[]{:S(2)}) collective-permute-start(bf16[1,200,768]{2,1,0:T(8,128)(2,1)S(1)} %slice.86), channel_id=1, source_target_pairs={{0,6},{2,0},{4,2},{6,4},{1,7},{3,1},{5,3},{7,5},{8,14},{10,8},{12,... | collective-permute-start | bytes 921608 | tf_op jit(solution)/shard_map/ppermute | solution.py:388
  55.9 12.4 %copy-start.9 = (f32[768]{0:T(1024)S(1)}, f32[768]{0:T(1024)}, u32[]{:S(2)}) copy-start(f32[768]{0:T(1024)} %param.12) | copy-start | bytes 9220
  55.9 7.2 %collective-permute-start = (bf16[4,32,768]{2,0,1:T(4,128)(2,1)S(1)}, bf16[4,32,768]{2,0,1:T(4,128)(2,1)S(1)}, u32[]{:S(2)}, u32[]{:S(2)}) collective-permute-start(bf16[4,32,768]{2,0,1:T(4,128)(2,1)S(1)} %fusion.7), channel_id=1, source_target_pairs={{0,1},{1,0},{2,3},{3,2},{4,5},{5,4},{6,7},{7,6},{8,9},{9,8},{10,11... | collective-permute-start | bytes 589832 | tf_op jit(solution)/shard_map/ppermute | solution.py:403
  57.1 32.2 %collective-permute-start.12 = (bf16[4,200,768]{2,1,0:T(8,128)(2,1)}, bf16[4,200,768]{2,1,0:T(8,128)(2,1)}, u32[]{:S(2)}, u32[]{:S(2)}) collective-permute-start(bf16[4,200,768]{2,1,0:T(8,128)(2,1)} %constant_dynamic-update-slice_fusion.3.rest_5_), channel_id=1, source_target_pairs={{0,6},{2,0},{4,2},{6,4},{1,7},{3,1},{5,3},{7,5},{8,14},{10,8},{12,... | collective-permute-start | bytes 3686408 | tf_op jit(solution)/shard_map/ppermute | solution.py:388
  62.6 31.4 %collective-permute-start.6 = (bf16[4,200,768]{2,1,0:T(8,128)(2,1)}, bf16[4,200,768]{2,1,0:T(8,128)(2,1)}, u32[]{:S(2)}, u32[]{:S(2)}) collective-permute-start(bf16[4,200,768]{2,1,0:T(8,128)(2,1)} %constant_dynamic-update-slice_fusion.rest_1_), channel_id=1, source_target_pairs={{0,24},{8,0},{16,8},{24,16},{1,25},{9,1},{17,9},{25,17},{2,26},{10... | collective-permute-start | bytes 3686408 | tf_op jit(solution)/shard_map/ppermute | solution.py:388
  63.1 53.8 %collective-permute-start.14 = (bf16[4,200,768]{2,1,0:T(8,128)(2,1)S(1)}, bf16[4,200,768]{2,1,0:T(8,128)(2,1)}, u32[]{:S(2)}, u32[]{:S(2)}) collective-permute-start(bf16[4,200,768]{2,1,0:T(8,128)(2,1)S(1)} %pad_maximum_fusion.rest_0_), channel_id=1, source_target_pairs={{0,24},{8,0},{16,8},{24,16},{1,25},{9,1},{17,9},{25,17},{2,26},{10... | collective-permute-start | bytes 3686408 | tf_op jit(solution)/shard_map/ppermute | solution.py:388
  63.2 53.7 %collective-permute-start.16 = (bf16[4,200,768]{2,1,0:T(8,128)(2,1)}, bf16[4,200,768]{2,1,0:T(8,128)(2,1)}, u32[]{:S(2)}, u32[]{:S(2)}) collective-permute-start(bf16[4,200,768]{2,1,0:T(8,128)(2,1)} %pad_maximum_fusion.1.rest_4_), channel_id=1, source_target_pairs={{0,6},{2,0},{4,2},{6,4},{1,7},{3,1},{5,3},{7,5},{8,14},{10,8},{12,... | collective-permute-start | bytes 3686408 | tf_op jit(solution)/shard_map/ppermute | solution.py:388
  65.1 53.9 %collective-permute-start.13 = (bf16[4,200,768]{2,1,0:T(8,128)(2,1)}, bf16[4,200,768]{2,1,0:T(8,128)(2,1)}, u32[]{:S(2)}, u32[]{:S(2)}) collective-permute-start(bf16[4,200,768]{2,1,0:T(8,128)(2,1)} %constant_dynamic-update-slice_fusion.rest_1_), channel_id=1, source_target_pairs={{0,8},{8,16},{16,24},{24,0},{1,9},{9,17},{17,25},{25,1},{2,10},{10... | collective-permute-start | bytes 3686408 | tf_op jit(solution)/shard_map/ppermute | solution.py:388
  89.3 50.9 %collective-permute-start.15 = (bf16[4,200,768]{2,1,0:T(8,128)(2,1)}, bf16[4,200,768]{2,1,0:T(8,128)(2,1)}, u32[]{:S(2)}, u32[]{:S(2)}) collective-permute-start(bf16[4,200,768]{2,1,0:T(8,128)(2,1)} %constant_dynamic-update-slice_fusion.3.rest_5_), channel_id=1, source_target_pairs={{0,2},{2,4},{4,6},{6,0},{1,3},{3,5},{5,7},{7,1},{8,10},{10,12},{12... | collective-permute-start | bytes 3686408 | tf_op jit(solution)/shard_map/ppermute | solution.py:388
  94.0 56.9 %collective-permute-start.17 = (bf16[4,200,768]{2,1,0:T(8,128)(2,1)}, bf16[4,200,768]{2,1,0:T(8,128)(2,1)S(1)}, u32[]{:S(2)}, u32[]{:S(2)}) collective-permute-start(bf16[4,200,768]{2,1,0:T(8,128)(2,1)} %collective-permute-done.2.rest_2_), channel_id=1, source_target_pairs={{0,8},{8,16},{16,24},{24,0},{1,9},{9,17},{17,25},{25,1},{2,10},{10... | collective-permute-start | bytes 3686408 | tf_op jit(solution)/shard_map/ppermute | solution.py:388
  116.9 34.0 %collective-permute-start.18 = (bf16[4,200,768]{2,1,0:T(8,128)(2,1)}, bf16[4,200,768]{2,1,0:T(8,128)(2,1)S(1)}, u32[]{:S(2)}, u32[]{:S(2)}) collective-permute-start(bf16[4,200,768]{2,1,0:T(8,128)(2,1)} %collective-permute-done.6.rest_3_), channel_id=1, source_target_pairs={{0,24},{8,0},{16,8},{24,16},{1,25},{9,1},{17,9},{25,17},{2,26},{10... | collective-permute-start | bytes 3686408 | tf_op jit(solution)/shard_map/ppermute | solution.py:388
  116.9 34.0 %collective-permute-start.19 = (bf16[4,200,768]{2,1,0:T(8,128)(2,1)}, bf16[4,200,768]{2,1,0:T(8,128)(2,1)}, u32[]{:S(2)}, u32[]{:S(2)}) collective-permute-start(bf16[4,200,768]{2,1,0:T(8,128)(2,1)} %collective-permute-done.8.rest_6_), channel_id=1, source_target_pairs={{0,2},{2,4},{4,6},{6,0},{1,3},{3,5},{5,7},{7,1},{8,10},{10,12},{12... | collective-permute-start | bytes 3686408 | tf_op jit(solution)/shard_map/ppermute | solution.py:388
  119.0 31.9 %collective-permute-start.20 = (bf16[4,200,768]{2,1,0:T(8,128)(2,1)}, bf16[4,200,768]{2,1,0:T(8,128)(2,1)}, u32[]{:S(2)}, u32[]{:S(2)}) collective-permute-start(bf16[4,200,768]{2,1,0:T(8,128)(2,1)} %collective-permute-done.12.rest_7_), channel_id=1, source_target_pairs={{0,6},{2,0},{4,2},{6,4},{1,7},{3,1},{5,3},{7,5},{8,14},{10,8},{12,... | collective-permute-start | bytes 3686408 | tf_op jit(solution)/shard_map/ppermute | solution.py:388
  172.0 19.7 %collective-permute-start.21 = (f32[768,768]{1,0:T(8,128)}, f32[768,768]{1,0:T(8,128)S(1)}, u32[]{:S(2)}, u32[]{:S(2)}) collective-permute-start(f32[768,768]{1,0:T(8,128)} %get-tuple-element.58), channel_id=1, source_target_pairs={{0,1},{1,0},{2,3},{3,2},{4,5},{5,4},{6,7},{7,6},{8,9},{9,8},{10,11... | collective-permute-start | bytes 7077896 | tf_op jit(solution)/shard_map/ppermute | solution.py:403
  172.1 5.3 %collective-permute-start.25 = (f32[136,768]{1,0:T(8,128)}, f32[136,768]{1,0:T(8,128)S(1)}, u32[]{:S(2)}, u32[]{:S(2)}) collective-permute-start(f32[136,768]{1,0:T(8,128)} %get-tuple-element.60), channel_id=1, source_target_pairs={{0,1},{1,0},{2,3},{3,2},{4,5},{5,4},{6,7},{7,6},{8,9},{9,8},{10,11... | collective-permute-start | bytes 1253384 | tf_op jit(solution)/shard_map/ppermute | solution.py:403
  181.6 3.4 %collective-permute-start.26 = (f32[384,768]{1,0:T(8,128)}, f32[384,768]{1,0:T(8,128)S(1)}, u32[]{:S(2)}, u32[]{:S(2)}) collective-permute-start(f32[384,768]{1,0:T(8,128)} %get-tuple-element.65), channel_id=1, source_target_pairs={{0,1},{1,0},{2,3},{3,2},{4,5},{5,4},{6,7},{7,6},{8,9},{9,8},{10,11... | collective-permute-start | bytes 3538952 | tf_op jit(solution)/shard_map/ppermute | solution.py:403
  186.7 20.6 %collective-permute-start.27 = (f32[96,768]{1,0:T(8,128)S(1)}, f32[96,768]{1,0:T(8,128)S(1)}, u32[]{:S(2)}, u32[]{:S(2)}) collective-permute-start(f32[96,768]{1,0:T(8,128)S(1)} %get-tuple-element.74), channel_id=1, source_target_pairs={{0,32},{32,64},{64,96},{96,0},{1,33},{33,65},{65,97},{97,1},{2,34}... | collective-permute-start | bytes 884744 | tf_op jit(solution)/shard_map/ppermute | solution.py:442
  187.6 26.5 %collective-permute-start.28 = (f32[96,768]{1,0:T(8,128)S(1)}, f32[96,768]{1,0:T(8,128)S(1)}, u32[]{:S(2)}, u32[]{:S(2)}) collective-permute-start(f32[96,768]{1,0:T(8,128)S(1)} %get-tuple-element.76), channel_id=1, source_target_pairs={{0,64},{32,96},{64,0},{96,32},{1,65},{33,97},{65,1},{97,33},{2,66}... | collective-permute-start | bytes 884744 | tf_op jit(solution)/shard_map/ppermute | solution.py:442
  191.7 22.5 %collective-permute-start.29 = (f32[96,768]{1,0:T(8,128)S(1)}, f32[96,768]{1,0:T(8,128)S(1)}, u32[]{:S(2)}, u32[]{:S(2)}) collective-permute-start(f32[96,768]{1,0:T(8,128)S(1)} %get-tuple-element.75), channel_id=1, source_target_pairs={{0,96},{32,0},{64,32},{96,64},{1,97},{33,1},{65,33},{97,65},{2,98}... | collective-permute-start | bytes 884744 | tf_op jit(solution)/shard_map/ppermute | solution.py:442
  192.1 23.8 %collective-permute-start.22 = (f32[96,768]{1,0:T(8,128)S(1)}, f32[96,768]{1,0:T(8,128)S(1)}, u32[]{:S(2)}, u32[]{:S(2)}) collective-permute-start(f32[96,768]{1,0:T(8,128)S(1)} %get-tuple-element.77), channel_id=1, source_target_pairs={{0,2},{2,4},{4,6},{6,0},{1,3},{3,5},{5,7},{7,1},{8,10},{10,12},{12... | collective-permute-start | bytes 884744 | tf_op jit(solution)/shard_map/ppermute | solution.py:442
  201.6 20.6 %collective-permute-start.23 = (f32[96,768]{1,0:T(8,128)S(1)}, f32[96,768]{1,0:T(8,128)S(1)}, u32[]{:S(2)}, u32[]{:S(2)}) collective-permute-start(f32[96,768]{1,0:T(8,128)S(1)} %get-tuple-element.79), channel_id=1, source_target_pairs={{0,4},{2,6},{4,0},{6,2},{1,5},{3,7},{5,1},{7,3},{8,12},{10,14},{12... | collective-permute-start | bytes 884744 | tf_op jit(solution)/shard_map/ppermute | solution.py:442
  207.3 14.9 %collective-permute-start.24 = (f32[96,768]{1,0:T(8,128)S(1)}, f32[96,768]{1,0:T(8,128)S(1)}, u32[]{:S(2)}, u32[]{:S(2)}) collective-permute-start(f32[96,768]{1,0:T(8,128)S(1)} %get-tuple-element.78), channel_id=1, source_target_pairs={{0,6},{2,0},{4,2},{6,4},{1,7},{3,1},{5,3},{7,5},{8,14},{10,8},{12,... | collective-permute-start | bytes 884744 | tf_op jit(solution)/shard_map/ppermute | solution.py:442
  214.3 13.8 %collective-permute-start.30 = (f32[96,768]{1,0:T(8,128)S(1)}, f32[96,768]{1,0:T(8,128)S(1)}, u32[]{:S(2)}, u32[]{:S(2)}) collective-permute-start(f32[96,768]{1,0:T(8,128)S(1)} %get-tuple-element.71), channel_id=1, source_target_pairs={{0,8},{8,16},{16,24},{24,0},{1,9},{9,17},{17,25},{25,1},{2,10},{10... | collective-permute-start | bytes 884744 | tf_op jit(solution)/shard_map/ppermute | solution.py:442
  214.4 13.8 %collective-permute-start.31 = (f32[96,768]{1,0:T(8,128)S(1)}, f32[96,768]{1,0:T(8,128)S(1)}, u32[]{:S(2)}, u32[]{:S(2)}) collective-permute-start(f32[96,768]{1,0:T(8,128)S(1)} %get-tuple-element.73), channel_id=1, source_target_pairs={{0,16},{8,24},{16,0},{24,8},{1,17},{9,25},{17,1},{25,9},{2,18},{10... | collective-permute-start | bytes 884744 | tf_op jit(solution)/shard_map/ppermute | solution.py:442
  215.9 14.7 %collective-permute-start.32 = (f32[96,768]{1,0:T(8,128)S(1)}, f32[96,768]{1,0:T(8,128)S(1)}, u32[]{:S(2)}, u32[]{:S(2)}) collective-permute-start(f32[96,768]{1,0:T(8,128)S(1)} %get-tuple-element.72), channel_id=1, source_target_pairs={{0,24},{8,0},{16,8},{24,16},{1,25},{9,1},{17,9},{25,17},{2,26},{10... | collective-permute-start | bytes 884744 | tf_op jit(solution)/shard_map/ppermute | solution.py:442
  222.3 20.0 %collective-permute-start.39 = (f32[24,768]{1,0:T(8,128)S(1)}, f32[24,768]{1,0:T(8,128)S(1)}, u32[]{:S(2)}, u32[]{:S(2)}) collective-permute-start(f32[24,768]{1,0:T(8,128)S(1)} %get-tuple-element.83), channel_id=1, source_target_pairs={{0,8},{8,16},{16,24},{24,0},{1,9},{9,17},{17,25},{25,1},{2,10},{10... | collective-permute-start | bytes 221192 | tf_op jit(solution)/shard_map/ppermute | solution.py:442
  222.9 21.6 %collective-permute-start.40 = (f32[24,768]{1,0:T(8,128)S(1)}, f32[24,768]{1,0:T(8,128)S(1)}, u32[]{:S(2)}, u32[]{:S(2)}) collective-permute-start(f32[24,768]{1,0:T(8,128)S(1)} %get-tuple-element.85), channel_id=1, source_target_pairs={{0,16},{8,24},{16,0},{24,8},{1,17},{9,25},{17,1},{25,9},{2,18},{10... | collective-permute-start | bytes 221192 | tf_op jit(solution)/shard_map/ppermute | solution.py:442
  228.1 12.6 %copy-start.11 = (f32[16,256]{1,0:T(8,128)S(1)}, f32[16,256]{1,0:T(8,128)}, u32[]{:S(2)}) copy-start(f32[16,256]{1,0:T(8,128)} %get-tuple-element.61) | copy-start | bytes 49156
  228.1 16.4 %collective-permute-start.41 = (f32[24,768]{1,0:T(8,128)S(1)}, f32[24,768]{1,0:T(8,128)S(1)}, u32[]{:S(2)}, u32[]{:S(2)}) collective-permute-start(f32[24,768]{1,0:T(8,128)S(1)} %get-tuple-element.84), channel_id=1, source_target_pairs={{0,24},{8,0},{16,8},{24,16},{1,25},{9,1},{17,9},{25,17},{2,26},{10... | collective-permute-start | bytes 221192 | tf_op jit(solution)/shard_map/ppermute | solution.py:442
  230.7 15.0 %collective-permute-start.33 = (f32[48,768]{1,0:T(8,128)S(1)}, f32[48,768]{1,0:T(8,128)S(1)}, u32[]{:S(2)}, u32[]{:S(2)}) collective-permute-start(f32[48,768]{1,0:T(8,128)S(1)} %get-tuple-element.80), channel_id=1, source_target_pairs={{0,2},{2,4},{4,6},{6,0},{1,3},{3,5},{5,7},{7,1},{8,10},{10,12},{12... | collective-permute-start | bytes 442376 | tf_op jit(solution)/shard_map/ppermute | solution.py:442
  240.8 7.1 %collective-permute-start.34 = (f32[48,768]{1,0:T(8,128)S(1)}, f32[48,768]{1,0:T(8,128)S(1)}, u32[]{:S(2)}, u32[]{:S(2)}) collective-permute-start(f32[48,768]{1,0:T(8,128)S(1)} %get-tuple-element.81), channel_id=1, source_target_pairs={{0,4},{2,6},{4,0},{6,2},{1,5},{3,7},{5,1},{7,3},{8,12},{10,14},{12... | collective-permute-start | bytes 442376 | tf_op jit(solution)/shard_map/ppermute | solution.py:442
  242.3 7.0 %collective-permute-start.35 = (f32[48,768]{1,0:T(8,128)S(1)}, f32[48,768]{1,0:T(8,128)S(1)}, u32[]{:S(2)}, u32[]{:S(2)}) collective-permute-start(f32[48,768]{1,0:T(8,128)S(1)} %get-tuple-element.82), channel_id=1, source_target_pairs={{0,6},{2,0},{4,2},{6,4},{1,7},{3,1},{5,3},{7,5},{8,14},{10,8},{12,... | collective-permute-start | bytes 442376 | tf_op jit(solution)/shard_map/ppermute | solution.py:442
  249.5 5.4 %collective-permute-start.36 = (f32[6,768]{1,0:T(8,128)S(1)}, f32[6,768]{1,0:T(8,128)S(1)}, u32[]{:S(2)}, u32[]{:S(2)}) collective-permute-start(f32[6,768]{1,0:T(8,128)S(1)} %get-tuple-element.91), channel_id=1, source_target_pairs={{0,8},{8,16},{16,24},{24,0},{1,9},{9,17},{17,25},{25,1},{2,10},{10... | collective-permute-start | bytes 55304 | tf_op jit(solution)/shard_map/ppermute | solution.py:442
  249.6 5.6 %collective-permute-start.37 = (f32[6,768]{1,0:T(8,128)S(1)}, f32[6,768]{1,0:T(8,128)S(1)}, u32[]{:S(2)}, u32[]{:S(2)}) collective-permute-start(f32[6,768]{1,0:T(8,128)S(1)} %get-tuple-element.93), channel_id=1, source_target_pairs={{0,16},{8,24},{16,0},{24,8},{1,17},{9,25},{17,1},{25,9},{2,18},{10... | collective-permute-start | bytes 55304 | tf_op jit(solution)/shard_map/ppermute | solution.py:442
  251.5 5.0 %collective-permute-start.38 = (f32[6,768]{1,0:T(8,128)S(1)}, f32[6,768]{1,0:T(8,128)S(1)}, u32[]{:S(2)}, u32[]{:S(2)}) collective-permute-start(f32[6,768]{1,0:T(8,128)S(1)} %get-tuple-element.92), channel_id=1, source_target_pairs={{0,24},{8,0},{16,8},{24,16},{1,25},{9,1},{17,9},{25,17},{2,26},{10... | collective-permute-start | bytes 55304 | tf_op jit(solution)/shard_map/ppermute | solution.py:442
  251.6 5.6 %collective-permute-start.42 = (f32[12,768]{1,0:T(8,128)S(1)}, f32[12,768]{1,0:T(8,128)S(1)}, u32[]{:S(2)}, u32[]{:S(2)}) collective-permute-start(f32[12,768]{1,0:T(8,128)S(1)} %get-tuple-element.86), channel_id=1, source_target_pairs={{0,32},{32,64},{64,96},{96,0},{1,33},{33,65},{65,97},{97,1},{2,34}... | collective-permute-start | bytes 110600 | tf_op jit(solution)/shard_map/ppermute | solution.py:442
  254.2 5.6 %collective-permute-start.43 = (f32[12,768]{1,0:T(8,128)S(1)}, f32[12,768]{1,0:T(8,128)S(1)}, u32[]{:S(2)}, u32[]{:S(2)}) collective-permute-start(f32[12,768]{1,0:T(8,128)S(1)} %get-tuple-element.87), channel_id=1, source_target_pairs={{0,64},{32,96},{64,0},{96,32},{1,65},{33,97},{65,1},{97,33},{2,66}... | collective-permute-start | bytes 110600 | tf_op jit(solution)/shard_map/ppermute | solution.py:442
  254.9 5.4 %collective-permute-start.44 = (f32[12,768]{1,0:T(8,128)S(1)}, f32[12,768]{1,0:T(8,128)S(1)}, u32[]{:S(2)}, u32[]{:S(2)}) collective-permute-start(f32[12,768]{1,0:T(8,128)S(1)} %get-tuple-element.88), channel_id=1, source_target_pairs={{0,96},{32,0},{64,32},{96,64},{1,97},{33,1},{65,33},{97,65},{2,98}... | collective-permute-start | bytes 110600 | tf_op jit(solution)/shard_map/ppermute | solution.py:442
  (11 other events, 53.4 us)
